TPU v7x, 32 devices: a whole 2x2x4 slice. The times are simulated.
32 devices in a mesh: grp: 2 (over y), ti: 4 (over x, core), tj: 4 (over z).
Axes of the slice: x: 2, y: 2, z: 4, core: 2. Of those that a mesh axis runs over, the one named last changes fastest.
Arguments:
- corpus: bfloat16 [2, 24576, 1024], P('grp', ('ti', 'tj')), may hold values from -64 to 64
- slot_of_row: int32 [2, 24576], P('grp', ('ti', 'tj')), may hold values from -1 to 24575, as said below
Outputs:
- max_similarity: float32 [2, 12288], P('grp', ('ti', 'tj'))
Inputs may be any that keep to these rules, and one draw needn't show every extreme that they name: `slot_of_row`: every value from 0 to 24575 appears exactly once; a row with value v lies on a device whose ti index is (v % 12288) // 3072; from one device at most 192 rows have values in one aligned group of 768 consecutive values, and some device sends exactly 192 to some group.
All inputs are finite; a program needn't handle non-finite values.
Results may differ from a plain program's by a relative error of at most 0.0009.
Values may be sent and summed in bfloat16 or wider, within the bound.
A program may use at most 64 MiB of HBM per device.

v0:
```python
import functools

import jax
import jax.numpy as jnp
from jax import lax
from jax.experimental import pallas as pl
from jax.experimental.pallas import tpu as pltpu
from jax.sharding import PartitionSpec as P

MESH = pl.DeviceIdType.MESH
NT = (((1,), (1,)), ((), ()))
NN = (((1,), (0,)), ((), ()))
CORES = 2
EPSILON = 1e-06


def dot(a, b, dims):
    return lax.dot_general(a, b, dims, preferred_element_type=jnp.float32)


def kernel(geo, slots_ref, corpus_ref, out_ref, spot, ids_src, send, send_ids, got, got_ids,
           picks, summed, raw, units, best, parts, s_send, s_recv, i_send, i_recv,
           b_send, b_recv, p_send, p_recv):
    ti_count, tj_count, count, features, sub, cap, chunks, parts_f = geo
    width = features // parts_f
    owners = 2 * tj_count
    xs = ti_count // CORES
    zs = tj_count // 2
    blk = sub * tj_count
    cluster = blk * ti_count
    step = sub // chunks
    g, ti, tj = lax.axis_index("grp"), lax.axis_index("ti"), lax.axis_index("tj")
    x, core = ti // CORES, ti % CORES
    zh, zl = tj // zs, tj % zs
    lin = g * tj_count + tj

    def dev(gg, tt, jj):
        return {"grp": gg, "ti": tt, "tj": jj}

    def owner_dev(k):
        d = lax.rem(lin + k, owners)
        return d, dev(d // tj_count, ti, lax.rem(d, tj_count))

    def row_dev(dx, dy):
        return dev(lax.rem(g + dy, 2), lax.rem(x + dx, xs) * CORES + core, tj)

    def col_dev(dc, dz):
        return dev(g, x * CORES + lax.rem(core + dc, CORES), zh * zs + lax.rem(zl + dz, zs))

    def final_dev(dx, dy):
        return dev(zh, lax.rem(x + dx, xs) * CORES + core, lax.rem(g + dy, 2) * zs + zl)

    def feeder_dev(dx, dy):
        return dev(dy, lax.rem(x + dx, xs) * CORES + core, g * zs + zl)

    barrier = pltpu.get_barrier_semaphore()
    greeted = 0
    targets = [owner_dev(k)[1] for k in range(1, owners)]
    targets += [row_dev(dx, dy) for dx in range(1, xs) for dy in range(2)]
    targets += [col_dev(dc, dz) for dc in range(1, CORES) for dz in range(zs)]
    targets += [final_dev(dx, dy) for dx in range(1, xs) for dy in range(2)]
    targets += [feeder_dev(dx, dy) for dx in range(1, xs) for dy in range(2)]
    for target in targets:
        pl.semaphore_signal(barrier, inc=1, device_id=target, device_id_type=MESH)
        greeted += 1

    v = slots_ref[...]
    member = v >= 0
    second = (v >= cluster).astype(jnp.int32)
    inblk = v - second * cluster - ti * blk
    s = jnp.zeros_like(v)
    for k in range(1, tj_count):
        s = s + (inblk >= k * sub).astype(jnp.int32)
    pos = inblk - s * sub
    s_hi = (s >= zs).astype(jnp.int32)
    owner = s_hi * tj_count + second * zs + s - s_hi * zs
    owner = jnp.where(member, owner, owners)
    piece = 256 if count % 256 == 0 else 128
    before = (
        lax.broadcasted_iota(jnp.int32, (piece, piece), 0)
        < lax.broadcasted_iota(jnp.int32, (piece, piece), 1)
    ).astype(jnp.bfloat16)
    carry = jnp.zeros((owners, 1), jnp.float32)
    owner_iota = lax.broadcasted_iota(jnp.int32, (owners, piece), 0)
    for p in range(count // piece):
        part = slice(p * piece, (p + 1) * piece)
        mine = owner_iota == owner[:, part]
        hot = mine.astype(jnp.float32)
        ranks = dot(hot.astype(jnp.bfloat16), before, NN) + carry
        carry = carry + jnp.sum(hot, axis=1, keepdims=True)
        rank = jnp.sum(jnp.where(mine, ranks, 0.0), axis=0, keepdims=True).astype(jnp.int32)
        spot[:, part] = jnp.where(member[:, part], owner[:, part] * cap + rank, owners * cap)
    line = lax.broadcasted_iota(jnp.int32, (16, count), 0)
    ids_src[...] = jnp.where(
        line == 0, pos >> 5, jnp.where(line == 1, pos & 31, (line == 2).astype(jnp.int32))
    ).astype(jnp.float32).astype(jnp.bfloat16)

    row_peers = [(dx, dy) for dx in range(xs) for dy in range(2)]
    col_peers = [(dc, dz) for dc in range(CORES) for dz in range(zs)]
    own = len(row_peers) - 1
    row_at = {peer: i - 1 if i else own for i, peer in enumerate(row_peers)}
    col_at = {peer: own + i for i, peer in enumerate(col_peers)}
    lanes = [pl.ds(f * width, width) for f in range(parts_f)]
    half = sub // 2

    def pick_of(k):
        d = lax.rem(lin + k, owners)
        return (
            spot[...] == d * cap + lax.broadcasted_iota(jnp.int32, (cap, count), 0)
        ).astype(jnp.float32).astype(jnp.bfloat16)

    def row_copy(k, f):
        return pltpu.make_async_remote_copy(
            send.at[k, :, lanes[f]], got.at[k, :, lanes[f]], s_send.at[k, f], s_recv.at[k, f],
            device_id=owner_dev(k)[1], device_id_type=MESH)

    def id_copy(k):
        return pltpu.make_async_remote_copy(
            send_ids.at[k], got_ids.at[k], i_send.at[k], i_recv.at[k],
            device_id=owner_dev(k)[1], device_id_type=MESH)

    def start_pair(k, f):
        if f == 0:
            id_copy(k).start()
        row_copy(k, f).start()

    def pack(f):
        def one(k, _):
            pick = pick_of(k)
            send[k, :, lanes[f]] = dot(pick, corpus_ref[0, :, lanes[f]], NN).astype(jnp.bfloat16)
            if f == 0:
                send_ids[k, :, :cap] = dot(ids_src[...], pick, NT).astype(jnp.bfloat16)

            @pl.when(k > 1)
            def _():
                start_pair(k - 1, f)
            return 0

        lax.fori_loop(1, owners, one, 0)
        pick = pick_of(0)
        got[0, :, lanes[f]] = dot(pick, corpus_ref[0, :, lanes[f]], NN).astype(jnp.bfloat16)
        if f == 0:
            got_ids[0, :, :cap] = dot(ids_src[...], pick, NT).astype(jnp.bfloat16)
        start_pair(owners - 1, f)

    def place(f):
        def one(k, first):
            if f == 0:
                line_ids = got_ids[k, :, :cap].astype(jnp.float32)
                where = (line_ids[0:1] * 32.0 + line_ids[1:2]).astype(jnp.int32)
                where = jnp.where(line_ids[2:3] > 0.5, where, sub)
                picks[k] = (
                    where == lax.broadcasted_iota(jnp.int32, (sub, cap), 0)
                ).astype(jnp.float32).astype(jnp.bfloat16)
            term = dot(picks[k], got[k, :, lanes[f]], NN)
            summed[...] = term if first else summed[...] + term

        def arrived(k, _):
            if f == 0:
                id_copy(k).wait_recv()
            row_copy(k, f).wait_recv()
            one(k, False)
            return 0

        one(0, True)
        lax.fori_loop(1, owners, arrived, 0)

    started, waited = [], set()

    def block_copy(source, target, f, h, device):
        area = (pl.ds(h * half, half), lanes[f])
        return pltpu.make_async_remote_copy(
            raw.at[(source,) + area], raw.at[(target,) + area],
            b_send.at[target, f, h], b_recv.at[target, f, h],
            device_id=device, device_id_type=MESH)

    def ship(source, target, f, h, device):
        copy = block_copy(source, target, f, h, device)
        copy.start()
        started.append(copy)

    def need(block, f, h):
        if (block, f, h) not in waited:
            waited.add((block, f, h))
            block_copy(own, block, f, h, row_dev(0, 1)).wait_recv()

    def launch(f):
        for n in range(2):
            for dx, dy in row_peers[1:]:
                if xs == 2 and dx and dy:
                    continue
                ship(own, row_at[(-dx) % xs, (-dy) % 2], f, 1 - n if dy else n, row_dev(dx, dy))
            for dc, dz in col_peers[1:]:
                if zs == 2 and dc and dz:
                    continue
                ship(own, col_at[(-dc) % CORES, (-dz) % zs], f, n, col_dev(dc, dz))

    def relay(f):
        if xs == 2:
            need(row_at[1, 0], f, 0)
            ship(row_at[1, 0], row_at[1, 1], f, 0, row_dev(0, 1))
            need(row_at[0, 1], f, 1)
            ship(row_at[0, 1], row_at[1, 1], f, 1, row_dev(1, 0))
        if zs == 2:
            for h in range(2):
                need(col_at[0, 1], f, h)
                ship(col_at[0, 1], col_at[1, 1], f, h, col_dev(1, 0))

    pl.semaphore_wait(barrier, greeted)
    ahead = 2
    for f in range(min(ahead, parts_f)):
        pack(f)
    for f in range(parts_f):
        place(f)
        raw[own, :, lanes[f]] = summed[...].astype(jnp.bfloat16)
        if f == 0:
            best[...] = jnp.full(best.shape, -2.0, jnp.float32)
        if f:
            relay(f - 1)
        launch(f)
        if f + ahead < parts_f:
            pack(f + ahead)

    def norm(block):
        for f in range(parts_f):
            for h in range(2):
                if block != own:
                    need(block, f, h)

        def one(n, _):
            area = pl.ds(pl.multiple_of(n * 128, 128), 128)
            wide = raw[block, area, :].astype(jnp.float32)
            squares = jnp.sum(wide * wide, axis=1, keepdims=True)
            units[block, area, :] = (wide * lax.rsqrt(squares + EPSILON)).astype(jnp.bfloat16)
            return 0

        lax.fori_loop(0, sub // 128, one, 0)

    def tile(row, i, col, diagonal=False):
        part = pl.ds(pl.multiple_of(i * step, step), step)
        scores = dot(units[own + col], units[row, part, :], NT)
        if diagonal:
            same = (
                lax.broadcasted_iota(jnp.int32, (sub, step), 0)
                == i * step + lax.broadcasted_iota(jnp.int32, (sub, step), 1)
            )
            scores = jnp.where(same, -2.0, scores)
        top = jnp.max(scores.reshape(sub // 8, 8, step), axis=0)
        best[row, i] = jnp.maximum(best[row, i], top)
        return 0

    norm(own)
    lax.fori_loop(0, chunks, lambda i, _: tile(own, i, 0, True), 0)
    relay(parts_f - 1)
    for col in range(1, len(col_peers)):
        norm(own + col)
        lax.fori_loop(0, chunks, lambda i, _, col=col: tile(own, i, col), 0)

    def part_copy(peer):
        return pltpu.make_async_remote_copy(
            best.at[row_at[peer]], parts.at[x * 2 + g],
            p_send.at[row_at[peer]], p_recv.at[x * 2 + g],
            device_id=final_dev(*peer), device_id_type=MESH)

    stays = zh == g

    @pl.when(stays)
    def _():
        parts[x * 2 + g] = best[own]

    @pl.when(jnp.logical_not(stays))
    def _():
        part_copy((0, 0)).start()

    order = [peer for peer in row_peers[1:] if not (peer[0] and peer[1])]
    order += [peer for peer in row_peers[1:] if peer[0] and peer[1]]
    total = chunks * len(col_peers)
    for peer in order:
        row = row_at[peer]
        norm(row)
        lax.fori_loop(
            0, total, lambda n, _, row=row: tile(row, n // len(col_peers), n % len(col_peers)), 0)
        part_copy(peer).start()

    for feeder in range(len(row_peers)):
        arrived = pltpu.make_async_remote_copy(
            best.at[0], parts.at[feeder], p_send.at[0], p_recv.at[feeder],
            device_id=row_dev(0, 1), device_id_type=MESH)
        here = jnp.logical_and(stays, x * 2 + g == feeder)

        @pl.when(jnp.logical_not(here))
        def _(arrived=arrived):
            arrived.wait_recv()
    for i in range(chunks):
        top = jnp.max(parts[:, i], axis=0)
        out_ref[:, i * step : (i + 1) * step] = jnp.max(top, axis=0, keepdims=True)

    @pl.when(jnp.logical_not(stays))
    def _():
        part_copy((0, 0)).wait_send()

    for peer in row_peers[1:]:
        part_copy(peer).wait_send()
    for copy in started:
        copy.wait_send()

    def drain(k, _):
        id_copy(k).wait_send()
        for f in range(parts_f):
            row_copy(k, f).wait_send()
        return 0

    lax.fori_loop(1, owners, drain, 0)


def per_device(corpus, slot_of_row):
    ti_count, tj_count = lax.axis_size("ti"), lax.axis_size("tj")
    _, count, features = corpus.shape
    sub = count // 2
    cap = sub // tj_count
    owners = 2 * tj_count
    chunks, parts_f = 1, 4
    step = sub // chunks
    row_blocks, col_blocks = ti_count // CORES * 2, tj_count // 2 * CORES
    blocks = row_blocks + col_blocks - 1
    wide_cap = -(-cap // 128) * 128
    dma = pltpu.SemaphoreType.DMA
    vmem = pl.BlockSpec(memory_space=pltpu.VMEM)
    return pl.pallas_call(
        functools.partial(kernel, (ti_count, tj_count, count, features, sub, cap, chunks, parts_f)),
        out_shape=jax.ShapeDtypeStruct((1, sub), jnp.float32),
        in_specs=[vmem, vmem],
        out_specs=vmem,
        scratch_shapes=[
            pltpu.VMEM((1, count), jnp.int32),
            pltpu.VMEM((16, count), jnp.bfloat16),
            pltpu.VMEM((owners, cap, features), jnp.bfloat16),
            pltpu.VMEM((owners, 16, wide_cap), jnp.bfloat16),
            pltpu.VMEM((owners, cap, features), jnp.bfloat16),
            pltpu.VMEM((owners, 16, wide_cap), jnp.bfloat16),
            pltpu.VMEM((owners, sub, cap), jnp.bfloat16),
            pltpu.VMEM((sub, features // parts_f), jnp.float32),
            pltpu.VMEM((blocks, sub, features), jnp.bfloat16),
            pltpu.VMEM((blocks, sub, features), jnp.bfloat16),
            pltpu.VMEM((row_blocks, chunks, 8, step), jnp.float32),
            pltpu.VMEM((row_blocks, chunks, 8, step), jnp.float32),
            dma((owners, parts_f)), dma((owners, parts_f)), dma((owners,)), dma((owners,)),
            dma((blocks, parts_f, 2)), dma((blocks, parts_f, 2)),
            dma((row_blocks,)), dma((row_blocks,)),
        ],
        compiler_params=pltpu.CompilerParams(
            collective_id=0, has_side_effects=True, vmem_limit_bytes=60 * 1024 * 1024),
    )(slot_of_row, corpus)


def solution(mesh):
    in_specs = (P("grp", ("ti", "tj"), None), P("grp", ("ti", "tj")))
    out_specs = P("grp", ("ti", "tj"))
    return jax.shard_map(
        per_device, mesh=mesh, in_specs=in_specs, out_specs=out_specs, check_vma=False
    )
```

profile of v0, /device:TPU:0, one launch (start us, length us, event | category | flops | bytes accessed | tf_op | source)
XLA Modules:
  0.0 135.3 jit_solution(3790465182515970494)
XLA Ops:
  0.0 134.1 %shard_map.28 = f32[1,768]{1,0:T(1,128)} custom-call(s32[1,1536]{1,0:T(1,128)} %slots_ref.1, bf16[1,1536,1024]{2,1,0:T(8,128)(2,1)} %corpus_ref.1), custom_call_target="tpu_custom_call" | custom-call | tf_op jit(solution)/shard_map/pallas_call | solution.py:329
  134.1 1.3 copy.4
where the time goes:
time: 136 us; the launch traced here: 135 us
  Pallas kernels  134 us (99%)
    pallas_call x1, Pallas kernels, per_device(): pl.pallas_call(functools.partial(kernel, (ti_count, tj_count, count, feat...  134 us

commit v1 on v0

--- a/solution.py
+++ b/solution.py
@@ -353,9 +353,521 @@
     )(slot_of_row, corpus)
 
 
+def square_kernel(geo, slots_ref, corpus_ref, out_ref, rows, spot, ids_src, picks, send, send_ids,
+                  got, got_ids, wall, raw, acc, xbest, ybest, mine, parts,
+                  l_sem, d_send, d_recv, i_send, i_recv, g_send, g_recv, p_send, p_recv):
+    ti_count, tj_count, count, features, sub, cap, spans, phases = geo
+    groups = 2 * tj_count
+    homes = groups // 2
+    blk = sub * tj_count
+    cluster = blk * ti_count
+    g, ti, tj = lax.axis_index("grp"), lax.axis_index("ti"), lax.axis_index("tj")
+    x, core = ti // CORES, lax.rem(ti, CORES)
+    zh, zl = tj // 2, lax.rem(tj, 2)
+    lin = g * tj_count + tj
+    inner = zl != zh
+    outer = jnp.logical_not(inner)
+
+    def dev(gg, tt, jj):
+        return {"grp": gg, "ti": tt, "tj": jj}
+
+    def home(o):
+        half = o // 2
+        return lax.rem(o, 2), half * 2 + 1 - half
+
+    def at(dx, dc, dg=0):
+        xx = 1 - x if dx else x
+        cc = 1 - core if dc else core
+        return dev(1 - g if dg else g, xx * CORES + cc, tj)
+
+    pair_dev = dev(g, ti, zh * 2 + 1 - zl)
+    core_dev, x_dev, y_dev = at(0, 1), at(1, 0), at(0, 0, 1)
+
+    barrier = pltpu.get_barrier_semaphore()
+    devices = 2 * ti_count * tj_count
+    me = (g * ti_count + ti) * tj_count + tj
+
+    def greet(t, _):
+        other = lax.rem(me + t, devices)
+        pl.semaphore_signal(
+            barrier, inc=1, device_id_type=MESH,
+            device_id=dev(other // (ti_count * tj_count),
+                          lax.rem(other // tj_count, ti_count), lax.rem(other, tj_count)))
+        return 0
+
+    piece = 256 if count % 256 == 0 else 128
+    pieces = count // piece
+
+    def load(n):
+        area = pl.ds(n * piece, piece)
+        return pltpu.make_async_copy(corpus_ref.at[0, area, :], rows.at[area, :], l_sem.at[n])
+
+    for n in range(pieces):
+        load(n).start()
+    lax.fori_loop(1, devices, greet, 0)
+
+    v = slots_ref[...]
+    member = v >= 0
+    second = (v >= cluster).astype(jnp.int32)
+    inblk = v - second * cluster - ti * blk
+    s = jnp.zeros_like(v)
+    for k in range(1, tj_count):
+        s = s + (inblk >= k * sub).astype(jnp.int32)
+    pos = inblk - s * sub
+    group = jnp.where(member, second * tj_count + s, groups)
+    before = (
+        lax.broadcasted_iota(jnp.int32, (piece, piece), 0)
+        < lax.broadcasted_iota(jnp.int32, (piece, piece), 1)
+    ).astype(jnp.bfloat16)
+    carry = jnp.zeros((groups, 1), jnp.float32)
+    group_iota = lax.broadcasted_iota(jnp.int32, (groups, piece), 0)
+    for n in range(pieces):
+        part = slice(n * piece, (n + 1) * piece)
+        hits = group_iota == group[:, part]
+        hot = hits.astype(jnp.float32)
+        ranks = dot(hot.astype(jnp.bfloat16), before, NN) + carry
+        carry = carry + jnp.sum(hot, axis=1, keepdims=True)
+        rank = jnp.sum(jnp.where(hits, ranks, 0.0), axis=0, keepdims=True).astype(jnp.int32)
+        spot[:, part] = jnp.where(member[:, part], group[:, part] * cap + rank, groups * cap)
+    line = lax.broadcasted_iota(jnp.int32, (16, count), 0)
+    ids_src[...] = jnp.where(
+        line == 0, pos >> 5, jnp.where(line == 1, pos & 31, (line == 2).astype(jnp.int32))
+    ).astype(jnp.float32).astype(jnp.bfloat16)
+
+    def choose(q, _):
+        area = pl.ds(pl.multiple_of(q * cap, cap), cap)
+        pick = (
+            spot[...] == q * cap + lax.broadcasted_iota(jnp.int32, (cap, count), 0)
+        ).astype(jnp.float32).astype(jnp.bfloat16)
+        picks[area, :] = pick
+        send_ids[q, :, :cap] = dot(ids_src[...], pick, NT).astype(jnp.bfloat16)
+        return 0
+
+    lax.fori_loop(0, groups, choose, 0)
+
+    thin = piece // 2
+    for n in range(pieces):
+        load(n).wait()
+
+        def norm(m, _, n=n):
+            area = pl.ds(pl.multiple_of(n * piece + m * thin, thin), thin)
+            wide = rows[area, :].astype(jnp.float32)
+            squares = jnp.sum(wide * wide, axis=1, keepdims=True)
+            rows[area, :] = (wide * lax.rsqrt(squares + EPSILON)).astype(jnp.bfloat16)
+            return 0
+
+        lax.fori_loop(0, 2, norm, 0)
+
+    lanes = [pl.ds(a, b - a) for a, b in spans]
+    last = len(spans) - 1
+    far = (1 - zh) * (homes // 2)
+
+    def row_copy(o, src, f):
+        hg, hj = home(o)
+        return pltpu.make_async_remote_copy(
+            send.at[o, :, :, lanes[f]], got.at[:, pl.ds(pl.multiple_of(src * cap, cap), cap), lanes[f]],
+            d_send.at[o, f], d_recv.at[src, f], device_id=dev(hg, ti, hj), device_id_type=MESH)
+
+    def id_copy(o, src):
+        hg, hj = home(o)
+        return pltpu.make_async_remote_copy(
+            send_ids.at[pl.ds(o * 2, 2)], got_ids.at[src],
+            i_send.at[o], i_recv.at[src], device_id=dev(hg, ti, hj), device_id_type=MESH)
+
+    def is_me(o):
+        hg, hj = home(o)
+        return jnp.logical_and(hg == g, hj == tj)
+
+    def dispatch(o, fs):
+        @pl.when(is_me(o))
+        def _():
+            if fs[0] == 0:
+                pltpu.make_async_copy(
+                    send_ids.at[pl.ds(o * 2, 2)], got_ids.at[lin], i_recv.at[lin]).start()
+            for f in fs:
+                pltpu.make_async_copy(
+                    send.at[o, :, :, lanes[f]],
+                    got.at[:, pl.ds(pl.multiple_of(lin * cap, cap), cap), lanes[f]],
+                    d_recv.at[lin, f]).start()
+
+        @pl.when(jnp.logical_not(is_me(o)))
+        def _():
+            if fs[0] == 0:
+                id_copy(o, lin).start()
+            for f in fs:
+                row_copy(o, lin, f).start()
+
+    def pack(fs, j):
+        o = lax.rem(far + j, homes)
+        low, high = spans[fs[0]][0], spans[fs[-1]][1]
+        area = pl.ds(pl.multiple_of(o * 2 * cap, 2 * cap), 2 * cap)
+        chosen = dot(picks[area, :], rows[:, low:high], NN).astype(jnp.bfloat16)
+        send[o, :, :, low:high] = chosen.reshape(2, cap, high - low)
+
+    def pack_all(fs, first):
+        def one(j, _):
+            pack(fs, j)
+
+            @pl.when(j > 0)
+            def _():
+                dispatch(lax.rem(far + j - 1, homes), fs)
+            return 0
+
+        if first:
+            pack(fs, 0)
+            pl.semaphore_wait(barrier, devices - 1)
+            lax.fori_loop(1, homes, one, 0)
+        else:
+            lax.fori_loop(0, homes, one, 0)
+        dispatch(lax.rem(far + homes - 1, homes), fs)
+
+    runs, f = [], 0
+    while f <= last:
+        n = f + 1
+        while n <= last and spans[n][1] - spans[f][0] <= 256:
+            n += 1
+        runs.append(list(range(f, n)))
+        f = n
+    for i, fs in enumerate(runs):
+        pack_all(fs, i == 0)
+
+    xbest[...] = jnp.full(xbest.shape, -2.0, jnp.float32)
+    ybest[...] = jnp.full(ybest.shape, -2.0, jnp.float32)
+
+    def read_ids():
+        for src in range(groups):
+            id_copy(0, src).wait_recv()
+            for r in range(2):
+                wall[r, :, src * cap : (src + 1) * cap] = got_ids[src, r, :, :cap].astype(jnp.float32)
+        for r in range(2):
+            where = (wall[r, 0:1] * 32.0 + wall[r, 1:2]).astype(jnp.int32)
+            where = jnp.where(wall[r, 2:3] > 0.5, where, sub)
+
+            def one(n, _, r=r, where=where):
+                area = pl.ds(pl.multiple_of(r * sub + n * 128, 128), 128)
+                picks[area, :] = (
+                    where == n * 128 + lax.broadcasted_iota(jnp.int32, (128, count), 0)
+                ).astype(jnp.float32).astype(jnp.bfloat16)
+                return 0
+
+            lax.fori_loop(0, sub // 128, one, 0)
+
+    own, own_c, near_x, near_x_c, near_y, near_y_c, deep, deep_c = range(8)
+
+    def block_copy(source, target, f, device):
+        return pltpu.make_async_remote_copy(
+            raw.at[source, :, lanes[f]], raw.at[target, :, lanes[f]],
+            g_send.at[target, f], g_recv.at[target, f], device_id=device, device_id_type=MESH)
+
+    def arrive(target, f):
+        block_copy(own, target, f, core_dev).wait_recv()
+
+    step = sub // 2 if sub % 256 else 256
+
+    def place(f):
+        def arrived(src, _):
+            row_copy(0, src, f).wait_recv()
+            return 0
+
+        lax.fori_loop(0, groups, arrived, 0)
+        for r, target in ((1, deep), (0, own)):
+            def one(n, _, r=r, target=target):
+                area = pl.ds(pl.multiple_of(n * step, step), step)
+                chosen = picks[pl.ds(pl.multiple_of(r * sub + n * step, step), step), :]
+                raw[target, area, lanes[f]] = dot(chosen, got[r, :, lanes[f]], NN).astype(jnp.bfloat16)
+                return 0
+
+            lax.fori_loop(0, sub // step, one, 0)
+
+    def supply(f):
+        @pl.when(inner)
+        def _():
+            if f == 0:
+                read_ids()
+            place(f)
+            block_copy(deep, own, f, pair_dev).start()
+
+        @pl.when(outer)
+        def _():
+            arrive(own, f)
+
+        block_copy(own, near_y, f, y_dev).start()
+        block_copy(own, near_x, f, x_dev).start()
+        block_copy(own, own_c, f, core_dev).start()
+
+        @pl.when(inner)
+        def _():
+            block_copy(deep, deep_c, f, core_dev).start()
+
+    def forward(f):
+        arrive(near_y, f)
+
+        @pl.when(inner)
+        def _():
+            block_copy(near_y, deep, f, pair_dev).start()
+
+        block_copy(near_y, near_y_c, f, core_dev).start()
+        arrive(near_x, f)
+        block_copy(near_x, near_x_c, f, core_dev).start()
+
+    def collect_near(f):
+        arrive(own_c, f)
+
+        @pl.when(inner)
+        def _():
+            arrive(deep_c, f)
+
+    def collect_rest(f):
+        arrive(near_x_c, f)
+        arrive(near_y_c, f)
+
+        @pl.when(outer)
+        def _():
+            arrive(deep, f)
+
+    inner_jobs = [(own, own_c), (own, deep), (own, deep_c), (own, near_x), (near_x, deep), (near_x, deep_c),
+                  (own, near_y), (near_y, deep), (near_y, deep_c), (near_x, near_y)]
+    outer_jobs = [(own, own_c), (own, near_x), (own, near_y), (near_x, near_y), (deep, near_x), (deep, near_x_c)]
+    inner_early, outer_early = 3, 1
+
+    def shift(a, b):
+        if (a, b) == (own, near_x) or (a, b) == (near_x, near_y):
+            return x
+        return g if (a, b) == (own, near_y) else 0
+
+    def table(jobs, j):
+        a, b = 0, 0
+        for n, (p, q) in enumerate(jobs):
+            a = a + jnp.where(j == n, p, 0)
+            b = b + jnp.where(j == n, q + shift(p, q), 0)
+        return a, b
+
+    def tile(a, b, slot, n, phase, diagonal=False):
+        low, high = phases[phase]
+        part = pl.ds(pl.multiple_of(n * step, step), step)
+        scores = dot(raw[a, part, low:high], raw[b, :, low:high], NT)
+        if phase:
+            scores = scores + acc[slot, part, :]
+        if phase < len(phases) - 1:
+            acc[slot, part, :] = scores
+            return
+        if diagonal:
+            same = (
+                n * step + lax.broadcasted_iota(jnp.int32, (step, sub), 0)
+                == lax.broadcasted_iota(jnp.int32, (step, sub), 1)
+            )
+            scores = jnp.where(same, -2.0, scores)
+        xbest[b] = jnp.maximum(xbest[b], jnp.max(scores.reshape(step // 8, 8, sub), axis=0))
+        if diagonal:
+            return
+        side = scores[:, :128]
+        for k in range(1, sub // 128):
+            side = jnp.maximum(side, scores[:, k * 128 : (k + 1) * 128])
+        y = jnp.minimum(a // 2, 2)
+        ybest[y, part, :] = jnp.maximum(ybest[y, part, :], side)
+
+    per = sub // step
+
+    def diagonal(phase):
+        def one(n, _):
+            tile(own, own, 0, n, phase, True)
+            return 0
+
+        lax.fori_loop(0, per, one, 0)
+
+    def others(phase, start, stop):
+        def one(n, _):
+            j = n // per
+            ia, ib = table(inner_jobs, j)
+            oa, ob = table(outer_jobs, j)
+            tile(jnp.where(inner, ia, oa), jnp.where(inner, ib, ob), j + 1, lax.rem(n, per), phase)
+            return 0
+
+        lax.fori_loop(start * per, stop * per, one, 0)
+
+    skip = (lax.rem(x + g, 2) != core).astype(jnp.int32)
+    early = jnp.where(inner, inner_early, outer_early)
+    total = jnp.where(inner, len(inner_jobs), len(outer_jobs))
+
+    edges = [max(f for f in range(last + 1) if spans[f][1] <= high) for _, high in phases]
+    for f in range(last + 1):
+        supply(f)
+        if f:
+            forward(f - 1)
+        for phase, edge in enumerate(edges[:-1]):
+            if edge == f - 1:
+                for e in range(edges[phase - 1] + 1 if phase else 0, edge + 1):
+                    collect_near(e)
+                    collect_rest(e)
+                diagonal(phase)
+                others(phase, skip, total)
+    final = len(phases) - 1
+    left = range(edges[final - 1] + 1 if final else 0, last + 1)
+    diagonal(final)
+    for e in left:
+        collect_near(e)
+    others(final, skip, early)
+    forward(last)
+    for e in left:
+        collect_rest(e)
+    others(final, early, total)
+
+    sides = [ybest[0], ybest[1], ybest[2]]
+    tops = [jnp.max(jnp.transpose(side).reshape(16, 8, sub), axis=0) for side in sides]
+    y_of = {own: 0, near_x: 1}
+    for b in range(8):
+        top = xbest[b]
+        if b in y_of:
+            top = jnp.maximum(top, tops[y_of[b]])
+        if b == near_y:
+            top = jnp.maximum(top, jnp.where(inner, tops[2], -2.0))
+        if b == deep:
+            top = jnp.maximum(top, jnp.where(inner, -2.0, tops[2]))
+        mine[b] = jnp.max(top, axis=0, keepdims=True)
+
+    role = outer.astype(jnp.int32)
+
+    def final_dev(b):
+        dx, dc, dg = b in (near_x, near_x_c), b in (own_c, near_x_c, near_y_c, deep_c), b in (near_y, near_y_c)
+        gg = 1 - g if dg else g
+        rr = role
+        if b == deep:
+            gg = jnp.where(inner, g, 1 - g)
+        if b in (deep, deep_c):
+            rr = 1 - role
+        xx = 1 - x if dx else x
+        cc = 1 - core if dc else core
+        return zh, xx * CORES + cc, gg * 2 + rr
+
+    def part_copy(b):
+        gg, tt, jj = final_dev(b)
+        return pltpu.make_async_remote_copy(
+            mine.at[b], parts.at[b], p_send.at[b], p_recv.at[b],
+            device_id=dev(gg, tt, jj), device_id_type=MESH)
+
+    def stays(b):
+        gg, tt, jj = final_dev(b)
+        return jnp.logical_and(gg == g, jnp.logical_and(tt == ti, jj == tj))
+
+    def holds(b):
+        return inner if b == deep_c else True
+
+    for b in range(8):
+        @pl.when(jnp.logical_and(holds(b), stays(b)))
+        def _(b=b):
+            parts[b] = mine[b]
+
+        @pl.when(jnp.logical_and(holds(b), jnp.logical_not(stays(b))))
+        def _(b=b):
+            part_copy(b).start()
+
+    half, rr = tj // 2, lax.rem(tj, 2)
+
+    @pl.when(rr == 0)
+    def _():
+        parts[deep_c] = jnp.full((1, sub), -2.0, jnp.float32)
+
+    def giver(b):
+        dx, dc, dg = b in (near_x, near_x_c), b in (own_c, near_x_c, near_y_c, deep_c), b in (near_y, near_y_c)
+        gg = 1 - half if dg else half
+        plane = rr
+        if b == deep:
+            gg = jnp.where(rr == 0, 1 - half, half)
+        if b in (deep, deep_c):
+            plane = 1 - rr
+        xx = 1 - x if dx else x
+        cc = 1 - core if dc else core
+        zz = jnp.where(plane == 0, 1 - g, g)
+        return gg, xx * CORES + cc, g * 2 + zz
+
+    for b in range(8):
+        gg, tt, jj = giver(b)
+        here = jnp.logical_and(gg == g, jnp.logical_and(tt == ti, jj == tj))
+        comes = jnp.logical_not(here)
+        if b == deep_c:
+            comes = jnp.logical_and(comes, rr == 1)
+
+        @pl.when(comes)
+        def _(b=b):
+            part_copy(b).wait_recv()
+
+    out_ref[...] = jnp.max(parts[...], axis=0)
+
+    for b in range(8):
+        @pl.when(jnp.logical_and(holds(b), jnp.logical_not(stays(b))))
+        def _(b=b):
+            part_copy(b).wait_send()
+
+    def drain(o, _):
+        @pl.when(jnp.logical_not(is_me(o)))
+        def _():
+            id_copy(o, lin).wait_send()
+            for f in range(last + 1):
+                row_copy(o, lin, f).wait_send()
+        return 0
+
+    lax.fori_loop(0, homes, drain, 0)
+    for f in range(last + 1):
+        for target in (near_y, near_x, own_c, near_y_c, near_x_c):
+            block_copy(own, target, f, core_dev).wait_send()
+
+        @pl.when(inner)
+        def _(f=f):
+            for target in (own, deep_c, deep):
+                block_copy(own, target, f, core_dev).wait_send()
+
+
+def square(corpus, slot_of_row):
+    ti_count, tj_count = lax.axis_size("ti"), lax.axis_size("tj")
+    _, count, features = corpus.shape
+    sub = count // 2
+    cap = sub // tj_count
+    groups, homes = 2 * tj_count, tj_count
+    unit = features // 8
+    spans = [(0, 2 * unit), (2 * unit, 4 * unit), (4 * unit, 6 * unit), (6 * unit, 7 * unit), (7 * unit, features)]
+    phases = [(0, 4 * unit), (4 * unit, features)]
+    wide_cap = -(-cap // 128) * 128
+    jobs = 11
+    piece = 256 if count % 256 == 0 else 128
+    n = len(spans)
+    dma = pltpu.SemaphoreType.DMA
+    vmem = pl.BlockSpec(memory_space=pltpu.VMEM)
+    bf16, f32 = jnp.bfloat16, jnp.float32
+    return pl.pallas_call(
+        functools.partial(
+            square_kernel, (ti_count, tj_count, count, features, sub, cap, spans, phases)),
+        out_shape=jax.ShapeDtypeStruct((1, sub), f32),
+        in_specs=[vmem, pl.BlockSpec(memory_space=pl.ANY)],
+        out_specs=vmem,
+        scratch_shapes=[
+            pltpu.VMEM((count, features), bf16),
+            pltpu.VMEM((1, count), jnp.int32),
+            pltpu.VMEM((16, count), bf16),
+            pltpu.VMEM((count, count), bf16),
+            pltpu.VMEM((homes, 2, cap, features), bf16),
+            pltpu.VMEM((groups, 16, wide_cap), bf16),
+            pltpu.VMEM((2, groups * cap, features), bf16),
+            pltpu.VMEM((groups, 2, 16, wide_cap), bf16),
+            pltpu.VMEM((2, 16, count), f32),
+            pltpu.VMEM((8, sub, features), bf16),
+            pltpu.VMEM((jobs, sub, sub), f32),
+            pltpu.VMEM((8, 8, sub), f32),
+            pltpu.VMEM((3, sub, 128), f32),
+            pltpu.VMEM((8, 1, sub), f32),
+            pltpu.VMEM((8, 1, sub), f32),
+            dma((count // piece,)),
+            dma((homes, n)), dma((groups, n)), dma((homes,)), dma((groups,)),
+            dma((8, n)), dma((8, n)), dma((8,)), dma((8,)),
+        ],
+        compiler_params=pltpu.CompilerParams(
+            collective_id=1, has_side_effects=True, vmem_limit_bytes=62 * 1024 * 1024),
+    )(slot_of_row, corpus)
+
+
 def solution(mesh):
     in_specs = (P("grp", ("ti", "tj"), None), P("grp", ("ti", "tj")))
     out_specs = P("grp", ("ti", "tj"))
+    is_square = mesh.shape["ti"] == 2 * CORES and mesh.shape["tj"] == 4
     return jax.shard_map(
-        per_device, mesh=mesh, in_specs=in_specs, out_specs=out_specs, check_vma=False
+        square if is_square else per_device, mesh=mesh, in_specs=in_specs, out_specs=out_specs, check_vma=False
     )

time: 136 us -> 156 us (1.15)
  Pallas kernels: 134 us -> 154 us
    pallas_call x1, Pallas kernels: 134 us -> 154 us  [square(): pl.pallas_call(functools.partial(square_kernel, (ti_count, tj_count, coun...]
where the time goes in v1:
time: 156 us; the launch traced here: 155 us
  Pallas kernels  154 us (99%)
    pallas_call x1, Pallas kernels, square(): pl.pallas_call(functools.partial(square_kernel, (ti_count, tj_count, coun...  154 us

profile of v1, /device:TPU:0, one launch (start us, length us, event | category | flops | bytes accessed | tf_op | source)
XLA Modules:
  0.0 155.1 jit_solution(5051566077702569301)
XLA Ops:
  0.0 153.9 %shard_map.28 = f32[1,768]{1,0:T(1,128)} custom-call(s32[1,1536]{1,0:T(1,128)} %slots_ref.1, bf16[1,1536,1024]{2,1,0:T(8,128)(2,1)} %corpus_ref.1), custom_call_target="tpu_custom_call" | custom-call | tf_op jit(solution)/shard_map/pallas_call | solution.py:836
  153.9 1.3 copy.4

commit v2 on v1

--- a/solution.py
+++ b/solution.py
@@ -353,9 +353,9 @@
     )(slot_of_row, corpus)
 
 
-def square_kernel(geo, slots_ref, corpus_ref, out_ref, rows, spot, ids_src, picks, send, send_ids,
+def square_kernel(geo, slots_ref, corpus_ref, out_ref, rows, spot, ids_src, picks, send, send_ids, hop,
                   got, got_ids, wall, raw, acc, xbest, ybest, mine, parts,
-                  l_sem, d_send, d_recv, i_send, i_recv, g_send, g_recv, p_send, p_recv):
+                  l_sem, d_send, d_recv, h_send, h_recv, i_send, i_recv, g_send, g_recv, p_send, p_recv):
     ti_count, tj_count, count, features, sub, cap, spans, phases = geo
     groups = 2 * tj_count
     homes = groups // 2
@@ -440,7 +440,6 @@
             spot[...] == q * cap + lax.broadcasted_iota(jnp.int32, (cap, count), 0)
         ).astype(jnp.float32).astype(jnp.bfloat16)
         picks[area, :] = pick
-        send_ids[q, :, :cap] = dot(ids_src[...], pick, NT).astype(jnp.bfloat16)
         return 0
 
     lax.fori_loop(0, groups, choose, 0)
@@ -460,13 +459,27 @@
 
     lanes = [pl.ds(a, b - a) for a, b in spans]
     last = len(spans) - 1
-    far = (1 - zh) * (homes // 2)
+    lin_y = (1 - g) * tj_count + tj
+
+    def seat(src):
+        return pl.ds(pl.multiple_of(src * cap, cap), cap)
 
     def row_copy(o, src, f):
         hg, hj = home(o)
         return pltpu.make_async_remote_copy(
-            send.at[o, :, :, lanes[f]], got.at[:, pl.ds(pl.multiple_of(src * cap, cap), cap), lanes[f]],
+            send.at[o, :, :, lanes[f]], got.at[:, seat(src), lanes[f]],
             d_send.at[o, f], d_recv.at[src, f], device_id=dev(hg, ti, hj), device_id_type=MESH)
+
+    def hop_copy(o, half, f):
+        return pltpu.make_async_remote_copy(
+            send.at[o, :, :, lanes[f]], hop.at[half, :, :, lanes[f]],
+            d_send.at[o, f], h_recv.at[half, f], device_id=y_dev, device_id_type=MESH)
+
+    def relay_copy(half, f):
+        hg, hj = home(half * 2 + g)
+        return pltpu.make_async_remote_copy(
+            hop.at[half, :, :, lanes[f]], got.at[:, seat(lin_y), lanes[f]],
+            h_send.at[half, f], d_recv.at[lin_y, f], device_id=dev(hg, ti, hj), device_id_type=MESH)
 
     def id_copy(o, src):
         hg, hj = home(o)
@@ -478,58 +491,90 @@
         hg, hj = home(o)
         return jnp.logical_and(hg == g, hj == tj)
 
-    def dispatch(o, fs):
-        @pl.when(is_me(o))
-        def _():
-            if fs[0] == 0:
+    def level(half):
+        return home(half * 2)[1] == tj
+
+    halves = (1 - zh, zh)
+
+    def send_ids_out():
+        def one(o, _):
+            for q in (o * 2, o * 2 + 1):
+                pick = picks[pl.ds(pl.multiple_of(q * cap, cap), cap), :]
+                send_ids[q, :, :cap] = dot(ids_src[...], pick, NT).astype(jnp.bfloat16)
+
+            @pl.when(is_me(o))
+            def _():
                 pltpu.make_async_copy(
                     send_ids.at[pl.ds(o * 2, 2)], got_ids.at[lin], i_recv.at[lin]).start()
-            for f in fs:
+
+            @pl.when(jnp.logical_not(is_me(o)))
+            def _():
+                id_copy(o, lin).start()
+            return 0
+
+        lax.fori_loop(0, homes, one, 0)
+
+    def send_y(f, only=halves):
+        for half in only:
+            o = half * 2 + 1 - g
+
+            @pl.when(level(half))
+            def _(o=o):
+                row_copy(o, lin, f).start()
+
+            @pl.when(jnp.logical_not(level(half)))
+            def _(o=o, half=half):
+                hop_copy(o, half, f).start()
+
+    def send_z(f, only=halves):
+        for half in only:
+            o = half * 2 + g
+
+            @pl.when(level(half))
+            def _(o=o):
                 pltpu.make_async_copy(
-                    send.at[o, :, :, lanes[f]],
-                    got.at[:, pl.ds(pl.multiple_of(lin * cap, cap), cap), lanes[f]],
-                    d_recv.at[lin, f]).start()
-
-        @pl.when(jnp.logical_not(is_me(o)))
-        def _():
-            if fs[0] == 0:
-                id_copy(o, lin).start()
-            for f in fs:
+                    send.at[o, :, :, lanes[f]], got.at[:, seat(lin), lanes[f]], d_recv.at[lin, f]).start()
+
+            @pl.when(jnp.logical_not(level(half)))
+            def _(o=o):
                 row_copy(o, lin, f).start()
 
-    def pack(fs, j):
-        o = lax.rem(far + j, homes)
+    def relay(f):
+        for half in halves:
+            @pl.when(jnp.logical_not(level(half)))
+            def _(half=half):
+                hop_copy(half * 2, half, f).wait_recv()
+                relay_copy(half, f).start()
+
+    def pack(fs, first=0, stop=2):
         low, high = spans[fs[0]][0], spans[fs[-1]][1]
-        area = pl.ds(pl.multiple_of(o * 2 * cap, 2 * cap), 2 * cap)
-        chosen = dot(picks[area, :], rows[:, low:high], NN).astype(jnp.bfloat16)
-        send[o, :, :, low:high] = chosen.reshape(2, cap, high - low)
-
-    def pack_all(fs, first):
+
         def one(j, _):
-            pack(fs, j)
-
-            @pl.when(j > 0)
-            def _():
-                dispatch(lax.rem(far + j - 1, homes), fs)
+            half = lax.rem(1 - zh + j, 2)
+            area = pl.ds(pl.multiple_of(half * sub, sub), sub)
+            chosen = dot(picks[area, :], rows[:, low:high], NN).astype(jnp.bfloat16)
+            send[pl.ds(half * 2, 2), :, :, low:high] = chosen.reshape(2, 2, cap, high - low)
             return 0
 
-        if first:
-            pack(fs, 0)
-            pl.semaphore_wait(barrier, devices - 1)
-            lax.fori_loop(1, homes, one, 0)
-        else:
-            lax.fori_loop(0, homes, one, 0)
-        dispatch(lax.rem(far + homes - 1, homes), fs)
-
-    runs, f = [], 0
-    while f <= last:
-        n = f + 1
-        while n <= last and spans[n][1] - spans[f][0] <= 256:
-            n += 1
-        runs.append(list(range(f, n)))
-        f = n
-    for i, fs in enumerate(runs):
-        pack_all(fs, i == 0)
+        lax.fori_loop(first, stop, one, 0)
+
+    pack([0], 0, 1)
+    pl.semaphore_wait(barrier, devices - 1)
+    send_y(0, halves[:1])
+    send_z(0, halves[:1])
+    pack([0], 1, 2)
+    send_y(0, halves[1:])
+    send_z(0, halves[1:])
+    pack([1])
+    send_y(1)
+    send_ids_out()
+    pack([2])
+    relay(0)
+    send_z(1)
+    send_y(2)
+    pack([3, 4])
+    relay(1)
+    send_z(2)
 
     xbest[...] = jnp.full(xbest.shape, -2.0, jnp.float32)
     ybest[...] = jnp.full(ybest.shape, -2.0, jnp.float32)
@@ -552,7 +597,8 @@
 
             lax.fori_loop(0, sub // 128, one, 0)
 
-    own, own_c, near_x, near_x_c, near_y, near_y_c, deep, deep_c = range(8)
+    own, own_c, near_x, near_x_c, near_y, near_y_c, deep, deep_c, skew = range(9)
+    left, right = core == 0, core == 1
 
     def block_copy(source, target, f, device):
         return pltpu.make_async_remote_copy(
@@ -562,8 +608,6 @@
     def arrive(target, f):
         block_copy(own, target, f, core_dev).wait_recv()
 
-    step = sub // 2 if sub % 256 else 256
-
     def place(f):
         def arrived(src, _):
             row_copy(0, src, f).wait_recv()
@@ -571,13 +615,8 @@
 
         lax.fori_loop(0, groups, arrived, 0)
         for r, target in ((1, deep), (0, own)):
-            def one(n, _, r=r, target=target):
-                area = pl.ds(pl.multiple_of(n * step, step), step)
-                chosen = picks[pl.ds(pl.multiple_of(r * sub + n * step, step), step), :]
-                raw[target, area, lanes[f]] = dot(chosen, got[r, :, lanes[f]], NN).astype(jnp.bfloat16)
-                return 0
-
-            lax.fori_loop(0, sub // step, one, 0)
+            chosen = picks[r * sub : (r + 1) * sub, :]
+            raw[target, :, lanes[f]] = dot(chosen, got[r, :, lanes[f]], NN).astype(jnp.bfloat16)
 
     def supply(f):
         @pl.when(inner)
@@ -602,9 +641,13 @@
     def forward(f):
         arrive(near_y, f)
 
-        @pl.when(inner)
+        @pl.when(jnp.logical_and(inner, left))
         def _():
             block_copy(near_y, deep, f, pair_dev).start()
+
+        @pl.when(jnp.logical_and(inner, right))
+        def _():
+            block_copy(near_y, skew, f, x_dev).start()
 
         block_copy(near_y, near_y_c, f, core_dev).start()
         arrive(near_x, f)
@@ -621,7 +664,7 @@
         arrive(near_x_c, f)
         arrive(near_y_c, f)
 
-        @pl.when(outer)
+        @pl.when(jnp.logical_and(outer, left))
         def _():
             arrive(deep, f)
 
@@ -642,82 +685,104 @@
             b = b + jnp.where(j == n, q + shift(p, q), 0)
         return a, b
 
-    def tile(a, b, slot, n, phase, diagonal=False):
-        low, high = phases[phase]
-        part = pl.ds(pl.multiple_of(n * step, step), step)
-        scores = dot(raw[a, part, low:high], raw[b, :, low:high], NT)
-        if phase:
-            scores = scores + acc[slot, part, :]
+    def tile(a, b, slot, phase, diagonal=False):
+        low, high = phases[phase] if slot is not None else (0, features)
+        scores = dot(raw[a, :, low:high], raw[b, :, low:high], NT)
+        if phase and slot is not None:
+            scores = scores + acc[slot]
         if phase < len(phases) - 1:
-            acc[slot, part, :] = scores
+            acc[slot] = scores
             return
         if diagonal:
             same = (
-                n * step + lax.broadcasted_iota(jnp.int32, (step, sub), 0)
-                == lax.broadcasted_iota(jnp.int32, (step, sub), 1)
+                lax.broadcasted_iota(jnp.int32, (sub, sub), 0)
+                == lax.broadcasted_iota(jnp.int32, (sub, sub), 1)
             )
             scores = jnp.where(same, -2.0, scores)
-        xbest[b] = jnp.maximum(xbest[b], jnp.max(scores.reshape(step // 8, 8, sub), axis=0))
+        xbest[b] = jnp.maximum(xbest[b], jnp.max(scores.reshape(sub // 8, 8, sub), axis=0))
         if diagonal:
             return
         side = scores[:, :128]
         for k in range(1, sub // 128):
             side = jnp.maximum(side, scores[:, k * 128 : (k + 1) * 128])
-        y = jnp.minimum(a // 2, 2)
-        ybest[y, part, :] = jnp.maximum(ybest[y, part, :], side)
-
-    per = sub // step
+        y = 3 if slot is None else jnp.minimum(a // 2, 2)
+        ybest[y] = jnp.maximum(ybest[y], side)
 
     def diagonal(phase):
-        def one(n, _):
-            tile(own, own, 0, n, phase, True)
-            return 0
-
-        lax.fori_loop(0, per, one, 0)
+        tile(own, own, 0, phase, True)
 
     def others(phase, start, stop):
-        def one(n, _):
-            j = n // per
+        def one(j, _):
             ia, ib = table(inner_jobs, j)
             oa, ob = table(outer_jobs, j)
-            tile(jnp.where(inner, ia, oa), jnp.where(inner, ib, ob), j + 1, lax.rem(n, per), phase)
+            tile(jnp.where(inner, ia, oa), jnp.where(inner, ib, ob), j + 1, phase)
             return 0
 
-        lax.fori_loop(start * per, stop * per, one, 0)
+        lax.fori_loop(start, stop, one, 0)
 
     skip = (lax.rem(x + g, 2) != core).astype(jnp.int32)
     early = jnp.where(inner, inner_early, outer_early)
-    total = jnp.where(inner, len(inner_jobs), len(outer_jobs))
-
-    edges = [max(f for f in range(last + 1) if spans[f][1] <= high) for _, high in phases]
-    for f in range(last + 1):
-        supply(f)
-        if f:
-            forward(f - 1)
-        for phase, edge in enumerate(edges[:-1]):
-            if edge == f - 1:
-                for e in range(edges[phase - 1] + 1 if phase else 0, edge + 1):
-                    collect_near(e)
-                    collect_rest(e)
-                diagonal(phase)
-                others(phase, skip, total)
+    total = jnp.where(inner, len(inner_jobs), jnp.where(left, len(outer_jobs), len(outer_jobs) - 2))
+
+    def collect(f):
+        collect_near(f)
+        collect_rest(f)
+
+    def score(phase):
+        diagonal(phase)
+        others(phase, skip, total)
+
+    supply(0)
+    send_y(3)
+    send_y(4)
+    relay(2)
+    send_z(3)
+    send_z(4)
+    relay(3)
+    relay(4)
+    forward(0)
+    supply(1)
+    forward(1)
+    supply(2)
+    collect(0)
+    collect(1)
+    score(0)
+    forward(2)
+    supply(3)
+    forward(3)
     final = len(phases) - 1
-    left = range(edges[final - 1] + 1 if final else 0, last + 1)
+    if final == 2:
+        collect(2)
+        score(1)
+    supply(4)
     diagonal(final)
-    for e in left:
-        collect_near(e)
+    for f in range(3 if final == 2 else 2, 5):
+        collect_near(f)
     others(final, skip, early)
-    forward(last)
-    for e in left:
-        collect_rest(e)
+    forward(4)
+    for f in range(3 if final == 2 else 2, 5):
+        collect_rest(f)
     others(final, early, total)
 
-    sides = [ybest[0], ybest[1], ybest[2]]
+    def score_skew():
+        @pl.when(jnp.logical_and(inner, right))
+        def _():
+            for f in range(last + 1):
+                arrive(skew, f)
+
+            def one(n, _):
+                tile(skew, deep + n, None, final)
+                return 0
+
+            lax.fori_loop(0, 2, one, 0)
+
+    score_skew()
+    sides = [ybest[n] for n in range(4)]
     tops = [jnp.max(jnp.transpose(side).reshape(16, 8, sub), axis=0) for side in sides]
-    y_of = {own: 0, near_x: 1}
-    for b in range(8):
-        top = xbest[b]
-        if b in y_of:
+    y_of = {own: 0, near_x: 1, skew: 3}
+    for b in range(9):
+        top = tops[3] if b == skew else xbest[b]
+        if b in y_of and b != skew:
             top = jnp.maximum(top, tops[y_of[b]])
         if b == near_y:
             top = jnp.maximum(top, jnp.where(inner, tops[2], -2.0))
@@ -728,7 +793,7 @@
     role = outer.astype(jnp.int32)
 
     def final_dev(b):
-        dx, dc, dg = b in (near_x, near_x_c), b in (own_c, near_x_c, near_y_c, deep_c), b in (near_y, near_y_c)
+        dx, dc, dg = b in (near_x, near_x_c, skew), b in (own_c, near_x_c, near_y_c, deep_c), b in (near_y, near_y_c, skew)
         gg = 1 - g if dg else g
         rr = role
         if b == deep:
@@ -742,7 +807,8 @@
     def part_copy(b):
         gg, tt, jj = final_dev(b)
         return pltpu.make_async_remote_copy(
-            mine.at[b], parts.at[b], p_send.at[b], p_recv.at[b],
+            mine.at[b], parts.at[deep if b == skew else b], p_send.at[b],
+            p_recv.at[deep if b == skew else b],
             device_id=dev(gg, tt, jj), device_id_type=MESH)
 
     def stays(b):
@@ -750,12 +816,16 @@
         return jnp.logical_and(gg == g, jnp.logical_and(tt == ti, jj == tj))
 
     def holds(b):
-        return inner if b == deep_c else True
-
-    for b in range(8):
+        if b == deep_c:
+            return inner
+        if b == deep:
+            return jnp.logical_or(inner, left)
+        return jnp.logical_and(inner, right) if b == skew else True
+
+    for b in range(9):
         @pl.when(jnp.logical_and(holds(b), stays(b)))
         def _(b=b):
-            parts[b] = mine[b]
+            parts[deep if b == skew else b] = mine[b]
 
         @pl.when(jnp.logical_and(holds(b), jnp.logical_not(stays(b))))
         def _(b=b):
@@ -771,11 +841,13 @@
         dx, dc, dg = b in (near_x, near_x_c), b in (own_c, near_x_c, near_y_c, deep_c), b in (near_y, near_y_c)
         gg = 1 - half if dg else half
         plane = rr
+        xx = 1 - x if dx else x
         if b == deep:
             gg = jnp.where(rr == 0, 1 - half, half)
-        if b in (deep, deep_c):
+            xx = jnp.where(jnp.logical_and(rr == 0, right), 1 - x, x)
+            plane = jnp.where(jnp.logical_and(rr == 0, left), 1, 0)
+        if b == deep_c:
             plane = 1 - rr
-        xx = 1 - x if dx else x
         cc = 1 - core if dc else core
         zz = jnp.where(plane == 0, 1 - g, g)
         return gg, xx * CORES + cc, g * 2 + zz
@@ -793,7 +865,7 @@
 
     out_ref[...] = jnp.max(parts[...], axis=0)
 
-    for b in range(8):
+    for b in range(9):
         @pl.when(jnp.logical_and(holds(b), jnp.logical_not(stays(b))))
         def _(b=b):
             part_copy(b).wait_send()
@@ -807,14 +879,27 @@
         return 0
 
     lax.fori_loop(0, homes, drain, 0)
+    for half in halves:
+        @pl.when(jnp.logical_not(level(half)))
+        def _(half=half):
+            for f in range(last + 1):
+                relay_copy(half, f).wait_send()
     for f in range(last + 1):
         for target in (near_y, near_x, own_c, near_y_c, near_x_c):
             block_copy(own, target, f, core_dev).wait_send()
 
         @pl.when(inner)
         def _(f=f):
-            for target in (own, deep_c, deep):
+            for target in (own, deep_c):
                 block_copy(own, target, f, core_dev).wait_send()
+
+        @pl.when(jnp.logical_and(inner, left))
+        def _(f=f):
+            block_copy(own, deep, f, core_dev).wait_send()
+
+        @pl.when(jnp.logical_and(inner, right))
+        def _(f=f):
+            block_copy(own, skew, f, core_dev).wait_send()
 
 
 def square(corpus, slot_of_row):
@@ -825,7 +910,7 @@
     groups, homes = 2 * tj_count, tj_count
     unit = features // 8
     spans = [(0, 2 * unit), (2 * unit, 4 * unit), (4 * unit, 6 * unit), (6 * unit, 7 * unit), (7 * unit, features)]
-    phases = [(0, 4 * unit), (4 * unit, features)]
+    phases = [(0, 4 * unit), (4 * unit, 6 * unit), (6 * unit, features)]
     wide_cap = -(-cap // 128) * 128
     jobs = 11
     piece = 256 if count % 256 == 0 else 128
@@ -846,21 +931,22 @@
             pltpu.VMEM((count, count), bf16),
             pltpu.VMEM((homes, 2, cap, features), bf16),
             pltpu.VMEM((groups, 16, wide_cap), bf16),
+            pltpu.VMEM((2, 2, cap, features), bf16),
             pltpu.VMEM((2, groups * cap, features), bf16),
             pltpu.VMEM((groups, 2, 16, wide_cap), bf16),
             pltpu.VMEM((2, 16, count), f32),
-            pltpu.VMEM((8, sub, features), bf16),
+            pltpu.VMEM((9, sub, features), bf16),
             pltpu.VMEM((jobs, sub, sub), f32),
             pltpu.VMEM((8, 8, sub), f32),
-            pltpu.VMEM((3, sub, 128), f32),
-            pltpu.VMEM((8, 1, sub), f32),
+            pltpu.VMEM((4, sub, 128), f32),
+            pltpu.VMEM((9, 1, sub), f32),
             pltpu.VMEM((8, 1, sub), f32),
             dma((count // piece,)),
-            dma((homes, n)), dma((groups, n)), dma((homes,)), dma((groups,)),
-            dma((8, n)), dma((8, n)), dma((8,)), dma((8,)),
+            dma((homes, n)), dma((groups, n)), dma((2, n)), dma((2, n)), dma((homes,)), dma((groups,)),
+            dma((9, n)), dma((9, n)), dma((9,)), dma((8,)),
         ],
         compiler_params=pltpu.CompilerParams(
-            collective_id=1, has_side_effects=True, vmem_limit_bytes=62 * 1024 * 1024),
+            collective_id=1, has_side_effects=True, vmem_limit_bytes=63 * 1024 * 1024),
     )(slot_of_row, corpus)
 
 

time: 156 us -> 117 us (0.75)
  Pallas kernels: 154 us -> 115 us
    pallas_call x1, Pallas kernels: 154 us -> 115 us  [square(): pl.pallas_call(functools.partial(square_kernel, (ti_count, tj_count, coun...]
where the time goes in v2:
time: 117 us; the launch traced here: 116 us
  Pallas kernels  115 us (98%)
  local copies, waits for them, and re-layouts  1.26 us (1%)
    pallas_call x1, Pallas kernels, square(): pl.pallas_call(functools.partial(square_kernel, (ti_count, tj_count, coun...  115 us

profile of v2, /device:TPU:0, one launch (start us, length us, event | category | flops | bytes accessed | tf_op | source)
XLA Modules:
  0.0 116.4 jit_solution(9489301193045380122)
XLA Ops:
  0.0 115.2 %shard_map.28 = f32[1,768]{1,0:T(1,128)} custom-call(s32[1,1536]{1,0:T(1,128)} %slots_ref.1, bf16[1,1536,1024]{2,1,0:T(8,128)(2,1)} %corpus_ref.1), custom_call_target="tpu_custom_call" | custom-call | tf_op jit(solution)/shard_map/pallas_call | solution.py:921
  115.2 1.3 %copy.4 = f32[1,768]{1,0:T(1,128)} copy(f32[1,768]{1,0:T(1,128)} %shard_map.28) | data formatting | bytes 6144

commit v3 on v2

--- a/solution.py
+++ b/solution.py
@@ -356,7 +356,7 @@
 def square_kernel(geo, slots_ref, corpus_ref, out_ref, rows, spot, ids_src, picks, send, send_ids, hop,
                   got, got_ids, wall, raw, acc, xbest, ybest, mine, parts,
                   l_sem, d_send, d_recv, h_send, h_recv, i_send, i_recv, g_send, g_recv, p_send, p_recv):
-    ti_count, tj_count, count, features, sub, cap, spans, phases = geo
+    ti_count, tj_count, count, features, sub, cap, spans, cuts, phases = geo
     groups = 2 * tj_count
     homes = groups // 2
     blk = sub * tj_count
@@ -385,15 +385,6 @@
 
     barrier = pltpu.get_barrier_semaphore()
     devices = 2 * ti_count * tj_count
-    me = (g * ti_count + ti) * tj_count + tj
-
-    def greet(t, _):
-        other = lax.rem(me + t, devices)
-        pl.semaphore_signal(
-            barrier, inc=1, device_id_type=MESH,
-            device_id=dev(other // (ti_count * tj_count),
-                          lax.rem(other // tj_count, ti_count), lax.rem(other, tj_count)))
-        return 0
 
     piece = 256 if count % 256 == 0 else 128
     pieces = count // piece
@@ -404,7 +395,14 @@
 
     for n in range(pieces):
         load(n).start()
-    lax.fori_loop(1, devices, greet, 0)
+    for dg in range(2):
+        for dt in range(ti_count):
+            for dj in range(tj_count):
+                if dg or dt or dj:
+                    pl.semaphore_signal(
+                        barrier, inc=1, device_id_type=MESH,
+                        device_id=dev(1 - g if dg else g, lax.rem(ti + dt, ti_count),
+                                      lax.rem(tj + dj, tj_count)))
 
     v = slots_ref[...]
     member = v >= 0
@@ -558,23 +556,23 @@
 
         lax.fori_loop(first, stop, one, 0)
 
-    pack([0], 0, 1)
+    pack([0, 1], 0, 1)
     pl.semaphore_wait(barrier, devices - 1)
     send_y(0, halves[:1])
     send_z(0, halves[:1])
-    pack([0], 1, 2)
+    send_ids_out()
+    pack([0, 1], 1, 2)
     send_y(0, halves[1:])
     send_z(0, halves[1:])
-    pack([1])
     send_y(1)
-    send_ids_out()
     pack([2])
     relay(0)
     send_z(1)
     send_y(2)
-    pack([3, 4])
+    pack([3])
     relay(1)
     send_z(2)
+    pack([4, 5])
 
     xbest[...] = jnp.full(xbest.shape, -2.0, jnp.float32)
     ybest[...] = jnp.full(ybest.shape, -2.0, jnp.float32)
@@ -600,58 +598,81 @@
     own, own_c, near_x, near_x_c, near_y, near_y_c, deep, deep_c, skew = range(9)
     left, right = core == 0, core == 1
 
-    def block_copy(source, target, f, device):
+    def block_copy(source, target, c, device):
+        f, start, size = cuts[c]
+        area = pl.ds(start, size)
         return pltpu.make_async_remote_copy(
-            raw.at[source, :, lanes[f]], raw.at[target, :, lanes[f]],
-            g_send.at[target, f], g_recv.at[target, f], device_id=device, device_id_type=MESH)
+            raw.at[source, area, lanes[f]], raw.at[target, area, lanes[f]],
+            g_send.at[target, c], g_recv.at[target, c], device_id=device, device_id_type=MESH)
+
+    def of(f):
+        return [c for c, cut in enumerate(cuts) if cut[0] == f]
 
     def arrive(target, f):
-        block_copy(own, target, f, core_dev).wait_recv()
-
-    def place(f):
-        def arrived(src, _):
-            row_copy(0, src, f).wait_recv()
-            return 0
-
-        lax.fori_loop(0, groups, arrived, 0)
-        for r, target in ((1, deep), (0, own)):
-            chosen = picks[r * sub : (r + 1) * sub, :]
-            raw[target, :, lanes[f]] = dot(chosen, got[r, :, lanes[f]], NN).astype(jnp.bfloat16)
-
-    def supply(f):
+        for c in of(f):
+            block_copy(own, target, c, core_dev).wait_recv()
+
+    def place(r, target, c):
+        f, start, size = cuts[c]
+        chosen = picks[r * sub + start : r * sub + start + size, :]
+        raw[target, start : start + size, lanes[f]] = dot(
+            chosen, got[r, :, lanes[f]], NN).astype(jnp.bfloat16)
+
+    def share(c):
+        block_copy(own, near_y, c, y_dev).start()
+        block_copy(own, near_x, c, x_dev).start()
+
+    def supply_inner(f):
         @pl.when(inner)
         def _():
             if f == 0:
                 read_ids()
-            place(f)
-            block_copy(deep, own, f, pair_dev).start()
-
+
+            def arrived(src, _):
+                row_copy(0, src, f).wait_recv()
+                return 0
+
+            lax.fori_loop(0, groups, arrived, 0)
+            for c in of(f):
+                place(1, deep, c)
+                place(0, own, c)
+                block_copy(deep, own, c, pair_dev).start()
+                share(c)
+            for c in of(f):
+                block_copy(deep, deep_c, c, core_dev).start()
+                block_copy(own, own_c, c, core_dev).start()
+
+    def supply_outer(f):
         @pl.when(outer)
         def _():
-            arrive(own, f)
-
-        block_copy(own, near_y, f, y_dev).start()
-        block_copy(own, near_x, f, x_dev).start()
-        block_copy(own, own_c, f, core_dev).start()
-
-        @pl.when(inner)
-        def _():
-            block_copy(deep, deep_c, f, core_dev).start()
+            for c in of(f):
+                block_copy(own, own, c, core_dev).wait_recv()
+                share(c)
+                block_copy(own, own_c, c, core_dev).start()
+
+    def supply(f):
+        supply_inner(f)
+        supply_outer(f)
 
     def forward(f):
-        arrive(near_y, f)
-
+        for c in of(f):
+            block_copy(own, near_y, c, core_dev).wait_recv()
+
+            @pl.when(jnp.logical_and(inner, right))
+            def _(c=c):
+                block_copy(near_y, skew, c, x_dev).start()
+
+            if f == last:
+                lower(c)
+            block_copy(near_y, near_y_c, c, core_dev).start()
+            block_copy(own, near_x, c, core_dev).wait_recv()
+            block_copy(near_x, near_x_c, c, core_dev).start()
+
+    def lower(*fs):
         @pl.when(jnp.logical_and(inner, left))
         def _():
-            block_copy(near_y, deep, f, pair_dev).start()
-
-        @pl.when(jnp.logical_and(inner, right))
-        def _():
-            block_copy(near_y, skew, f, x_dev).start()
-
-        block_copy(near_y, near_y_c, f, core_dev).start()
-        arrive(near_x, f)
-        block_copy(near_x, near_x_c, f, core_dev).start()
+            for c in fs:
+                block_copy(near_y, deep, c, pair_dev).start()
 
     def collect_near(f):
         arrive(own_c, f)
@@ -720,49 +741,75 @@
 
         lax.fori_loop(start, stop, one, 0)
 
-    skip = (lax.rem(x + g, 2) != core).astype(jnp.int32)
+    skip = jnp.where(inner, core, 1 - core)
     early = jnp.where(inner, inner_early, outer_early)
     total = jnp.where(inner, len(inner_jobs), jnp.where(left, len(outer_jobs), len(outer_jobs) - 2))
 
-    def collect(f):
-        collect_near(f)
-        collect_rest(f)
-
-    def score(phase):
+    def score_early(phase, *fs):
+        for f in fs:
+            collect_near(f)
         diagonal(phase)
-        others(phase, skip, total)
-
+        others(phase, skip, early)
+
+    def score_late(phase, *fs):
+        for f in fs:
+            collect_rest(f)
+        others(phase, early, total)
+
+    final = len(phases) - 1
     supply(0)
     send_y(3)
-    send_y(4)
     relay(2)
     send_z(3)
+    supply(1)
+    forward(0)
+    lower(0)
+    send_y(4)
+    relay(3)
     send_z(4)
-    relay(3)
-    relay(4)
-    forward(0)
-    supply(1)
+
+    @pl.when(outer)
+    def _():
+        send_y(5)
+
     forward(1)
     supply(2)
-    collect(0)
-    collect(1)
-    score(0)
+
+    @pl.when(inner)
+    def _():
+        send_y(5)
+
+    lower(1)
+    score_early(0, 0, 1, 2)
+    relay(4)
+    send_z(5)
+
+    @pl.when(outer)
+    def _():
+        relay(5)
+
     forward(2)
+    lower(2)
+
+    @pl.when(inner)
+    def _():
+        relay(5)
+
     supply(3)
+    supply_outer(4)
+    score_late(0, 0, 1, 2)
+    supply_inner(4)
+    score_early(1, 3)
+    supply_outer(5)
     forward(3)
-    final = len(phases) - 1
-    if final == 2:
-        collect(2)
-        score(1)
-    supply(4)
-    diagonal(final)
-    for f in range(3 if final == 2 else 2, 5):
-        collect_near(f)
-    others(final, skip, early)
+    lower(3)
+    score_late(1, 3)
+    supply_inner(5)
     forward(4)
-    for f in range(3 if final == 2 else 2, 5):
-        collect_rest(f)
-    others(final, early, total)
+    lower(4)
+    score_early(2, 4, 5)
+    forward(5)
+    score_late(2, 4, 5)
 
     def score_skew():
         @pl.when(jnp.logical_and(inner, right))
@@ -777,8 +824,10 @@
             lax.fori_loop(0, 2, one, 0)
 
     score_skew()
-    sides = [ybest[n] for n in range(4)]
-    tops = [jnp.max(jnp.transpose(side).reshape(16, 8, sub), axis=0) for side in sides]
+    tops = []
+    for n in range(4):
+        with_side = jnp.transpose(ybest[n])
+        tops.append(jnp.max(with_side.reshape(16, 8, sub), axis=0))
     y_of = {own: 0, near_x: 1, skew: 3}
     for b in range(9):
         top = tops[3] if b == skew else xbest[b]
@@ -884,22 +933,22 @@
         def _(half=half):
             for f in range(last + 1):
                 relay_copy(half, f).wait_send()
-    for f in range(last + 1):
+    for c in range(len(cuts)):
         for target in (near_y, near_x, own_c, near_y_c, near_x_c):
-            block_copy(own, target, f, core_dev).wait_send()
+            block_copy(own, target, c, core_dev).wait_send()
 
         @pl.when(inner)
-        def _(f=f):
+        def _(c=c):
             for target in (own, deep_c):
-                block_copy(own, target, f, core_dev).wait_send()
+                block_copy(own, target, c, core_dev).wait_send()
 
         @pl.when(jnp.logical_and(inner, left))
-        def _(f=f):
-            block_copy(own, deep, f, core_dev).wait_send()
+        def _(c=c):
+            block_copy(own, deep, c, core_dev).wait_send()
 
         @pl.when(jnp.logical_and(inner, right))
-        def _(f=f):
-            block_copy(own, skew, f, core_dev).wait_send()
+        def _(c=c):
+            block_copy(own, skew, c, core_dev).wait_send()
 
 
 def square(corpus, slot_of_row):
@@ -909,18 +958,20 @@
     cap = sub // tj_count
     groups, homes = 2 * tj_count, tj_count
     unit = features // 8
-    spans = [(0, 2 * unit), (2 * unit, 4 * unit), (4 * unit, 6 * unit), (6 * unit, 7 * unit), (7 * unit, features)]
+    edges = (0, 1, 2, 4, 6, 7, 8)
+    spans = [(a * unit, b * unit) for a, b in zip(edges, edges[1:])]
     phases = [(0, 4 * unit), (4 * unit, 6 * unit), (6 * unit, features)]
+    n = len(spans)
+    cuts = [(f, 0, sub) for f in range(n - 1)] + [(n - 1, 0, sub // 2), (n - 1, sub // 2, sub // 2)]
     wide_cap = -(-cap // 128) * 128
     jobs = 11
     piece = 256 if count % 256 == 0 else 128
-    n = len(spans)
     dma = pltpu.SemaphoreType.DMA
     vmem = pl.BlockSpec(memory_space=pltpu.VMEM)
     bf16, f32 = jnp.bfloat16, jnp.float32
     return pl.pallas_call(
         functools.partial(
-            square_kernel, (ti_count, tj_count, count, features, sub, cap, spans, phases)),
+            square_kernel, (ti_count, tj_count, count, features, sub, cap, spans, cuts, phases)),
         out_shape=jax.ShapeDtypeStruct((1, sub), f32),
         in_specs=[vmem, pl.BlockSpec(memory_space=pl.ANY)],
         out_specs=vmem,
@@ -943,7 +994,7 @@
             pltpu.VMEM((8, 1, sub), f32),
             dma((count // piece,)),
             dma((homes, n)), dma((groups, n)), dma((2, n)), dma((2, n)), dma((homes,)), dma((groups,)),
-            dma((9, n)), dma((9, n)), dma((9,)), dma((8,)),
+            dma((9, len(cuts))), dma((9, len(cuts))), dma((9,)), dma((8,)),
         ],
         compiler_params=pltpu.CompilerParams(
             collective_id=1, has_side_effects=True, vmem_limit_bytes=63 * 1024 * 1024),

time: 117 us -> 104 us (0.89)
  Pallas kernels: 115 us -> 102 us
    pallas_call x1, Pallas kernels: 115 us -> 102 us  [square(): pl.pallas_call(functools.partial(square_kernel, (ti_count, tj_count, coun...]
where the time goes in v3:
time: 104 us; the launch traced here: 103 us
  Pallas kernels  102 us (98%)
  local copies, waits for them, and re-layouts  1.26 us (1%)
    pallas_call x1, Pallas kernels, square(): pl.pallas_call(functools.partial(square_kernel, (ti_count, tj_count, coun...  102 us

profile of v3, /device:TPU:0, one launch (start us, length us, event | category | flops | bytes accessed | tf_op | source)
XLA Modules:
  0.0 103.3 jit_solution(9832482438878046411)
XLA Ops:
  0.0 102.1 %shard_map.28 = f32[1,768]{1,0:T(1,128)} custom-call(s32[1,1536]{1,0:T(1,128)} %slots_ref.1, bf16[1,1536,1024]{2,1,0:T(8,128)(2,1)} %corpus_ref.1), custom_call_target="tpu_custom_call" | custom-call | tf_op jit(solution)/shard_map/pallas_call | solution.py:972
  102.1 1.3 %copy.4 = f32[1,768]{1,0:T(1,128)} copy(f32[1,768]{1,0:T(1,128)} %shard_map.28) | data formatting | bytes 6144

commit v4 on v3

--- a/solution.py
+++ b/solution.py
@@ -355,8 +355,9 @@
 
 def square_kernel(geo, slots_ref, corpus_ref, out_ref, rows, spot, ids_src, picks, send, send_ids, hop,
                   got, got_ids, wall, raw, acc, xbest, ybest, mine, parts,
-                  l_sem, d_send, d_recv, h_send, h_recv, i_send, i_recv, g_send, g_recv, p_send, p_recv):
-    ti_count, tj_count, count, features, sub, cap, spans, cuts, phases = geo
+                  l_sem, d_send, d_recv, h_send, h_recv, i_send, i_recv, g_send, g_recv, f_recv,
+                  p_send, p_recv):
+    ti_count, tj_count, count, features, sub, cap, spans, units, cuts, phases = geo
     groups = 2 * tj_count
     homes = groups // 2
     blk = sub * tj_count
@@ -389,12 +390,8 @@
     piece = 256 if count % 256 == 0 else 128
     pieces = count // piece
 
-    def load(n):
-        area = pl.ds(n * piece, piece)
-        return pltpu.make_async_copy(corpus_ref.at[0, area, :], rows.at[area, :], l_sem.at[n])
-
-    for n in range(pieces):
-        load(n).start()
+    load = pltpu.make_async_copy(corpus_ref.at[0], rows, l_sem.at[0])
+    load.start()
     for dg in range(2):
         for dt in range(ti_count):
             for dj in range(tj_count):
@@ -443,17 +440,16 @@
     lax.fori_loop(0, groups, choose, 0)
 
     thin = piece // 2
-    for n in range(pieces):
-        load(n).wait()
-
-        def norm(m, _, n=n):
-            area = pl.ds(pl.multiple_of(n * piece + m * thin, thin), thin)
-            wide = rows[area, :].astype(jnp.float32)
-            squares = jnp.sum(wide * wide, axis=1, keepdims=True)
-            rows[area, :] = (wide * lax.rsqrt(squares + EPSILON)).astype(jnp.bfloat16)
-            return 0
-
-        lax.fori_loop(0, 2, norm, 0)
+    load.wait()
+
+    def norm(m, _):
+        area = pl.ds(pl.multiple_of(m * thin, thin), thin)
+        wide = rows[area, :].astype(jnp.float32)
+        squares = jnp.sum(wide * wide, axis=1, keepdims=True)
+        rows[area, :] = (wide * lax.rsqrt(squares + EPSILON)).astype(jnp.bfloat16)
+        return 0
+
+    lax.fori_loop(0, count // thin, norm, 0)
 
     lanes = [pl.ds(a, b - a) for a, b in spans]
     last = len(spans) - 1
@@ -462,28 +458,48 @@
     def seat(src):
         return pl.ds(pl.multiple_of(src * cap, cap), cap)
 
-    def row_copy(o, src, f):
+    def landed(ref, sem):
+        pltpu.make_async_remote_copy(
+            ref, ref, sem, sem, device_id=core_dev, device_id_type=MESH).wait_recv()
+
+    def departed(ref, sem):
+        pltpu.make_async_remote_copy(
+            ref, ref, sem, sem, device_id=core_dev, device_id_type=MESH).wait_send()
+
+    def row_copy(o, src, u):
+        f, half_block, size = units[u]
         hg, hj = home(o)
+        both = pl.ds(half_block, size)
         return pltpu.make_async_remote_copy(
-            send.at[o, :, :, lanes[f]], got.at[:, seat(src), lanes[f]],
-            d_send.at[o, f], d_recv.at[src, f], device_id=dev(hg, ti, hj), device_id_type=MESH)
-
-    def hop_copy(o, half, f):
+            send.at[o, both, :, lanes[f]], got.at[both, seat(src), lanes[f]],
+            d_send.at[o], d_recv.at[u], device_id=dev(hg, ti, hj), device_id_type=MESH)
+
+    def hop_copy(o, half, u):
+        f, half_block, size = units[u]
+        both = pl.ds(half_block, size)
         return pltpu.make_async_remote_copy(
-            send.at[o, :, :, lanes[f]], hop.at[half, :, :, lanes[f]],
-            d_send.at[o, f], h_recv.at[half, f], device_id=y_dev, device_id_type=MESH)
-
-    def relay_copy(half, f):
+            send.at[o, both, :, lanes[f]], hop.at[half, both, :, lanes[f]],
+            d_send.at[o], h_recv.at[half, u], device_id=y_dev, device_id_type=MESH)
+
+    def relay_copy(half, u):
+        f, half_block, size = units[u]
         hg, hj = home(half * 2 + g)
+        both = pl.ds(half_block, size)
         return pltpu.make_async_remote_copy(
-            hop.at[half, :, :, lanes[f]], got.at[:, seat(lin_y), lanes[f]],
-            h_send.at[half, f], d_recv.at[lin_y, f], device_id=dev(hg, ti, hj), device_id_type=MESH)
+            hop.at[half, both, :, lanes[f]], got.at[both, seat(lin_y), lanes[f]],
+            h_send.at[half], d_recv.at[u], device_id=dev(hg, ti, hj), device_id_type=MESH)
+
+    def stay_copy(o, u):
+        f, half_block, size = units[u]
+        both = pl.ds(half_block, size)
+        return pltpu.make_async_copy(
+            send.at[o, both, :, lanes[f]], got.at[both, seat(lin), lanes[f]], d_recv.at[u])
 
     def id_copy(o, src):
         hg, hj = home(o)
         return pltpu.make_async_remote_copy(
             send_ids.at[pl.ds(o * 2, 2)], got_ids.at[src],
-            i_send.at[o], i_recv.at[src], device_id=dev(hg, ti, hj), device_id_type=MESH)
+            i_send.at[o], i_recv.at[0], device_id=dev(hg, ti, hj), device_id_type=MESH)
 
     def is_me(o):
         hg, hj = home(o)
@@ -503,7 +519,7 @@
             @pl.when(is_me(o))
             def _():
                 pltpu.make_async_copy(
-                    send_ids.at[pl.ds(o * 2, 2)], got_ids.at[lin], i_recv.at[lin]).start()
+                    send_ids.at[pl.ds(o * 2, 2)], got_ids.at[lin], i_recv.at[0]).start()
 
             @pl.when(jnp.logical_not(is_me(o)))
             def _():
@@ -530,8 +546,7 @@
 
             @pl.when(level(half))
             def _(o=o):
-                pltpu.make_async_copy(
-                    send.at[o, :, :, lanes[f]], got.at[:, seat(lin), lanes[f]], d_recv.at[lin, f]).start()
+                stay_copy(o, f).start()
 
             @pl.when(jnp.logical_not(level(half)))
             def _(o=o):
@@ -569,6 +584,7 @@
     relay(0)
     send_z(1)
     send_y(2)
+    send_y(3)
     pack([3])
     relay(1)
     send_z(2)
@@ -578,8 +594,8 @@
     ybest[...] = jnp.full(ybest.shape, -2.0, jnp.float32)
 
     def read_ids():
+        landed(got_ids, i_recv.at[0])
         for src in range(groups):
-            id_copy(0, src).wait_recv()
             for r in range(2):
                 wall[r, :, src * cap : (src + 1) * cap] = got_ids[src, r, :, :cap].astype(jnp.float32)
         for r in range(2):
@@ -598,19 +614,28 @@
     own, own_c, near_x, near_x_c, near_y, near_y_c, deep, deep_c, skew = range(9)
     left, right = core == 0, core == 1
 
+    direct, passed = (own, near_x, near_y), (own_c, near_x_c, near_y_c, deep_c, deep, skew)
+
+    def phase_of(f):
+        return [n for n, (_, high) in enumerate(phases) if spans[f][1] <= high][0]
+
     def block_copy(source, target, c, device):
         f, start, size = cuts[c]
         area = pl.ds(start, size)
+        if target in direct:
+            sem = g_recv.at[direct.index(target), c]
+        else:
+            sem = f_recv.at[passed.index(target), phase_of(f)]
         return pltpu.make_async_remote_copy(
             raw.at[source, area, lanes[f]], raw.at[target, area, lanes[f]],
-            g_send.at[target, c], g_recv.at[target, c], device_id=device, device_id_type=MESH)
+            g_send.at[target], sem, device_id=device, device_id_type=MESH)
 
     def of(f):
         return [c for c, cut in enumerate(cuts) if cut[0] == f]
 
-    def arrive(target, f):
-        for c in of(f):
-            block_copy(own, target, c, core_dev).wait_recv()
+    def collect(target, phase):
+        low, high = phases[phase]
+        landed(raw.at[target, :, low:high], f_recv.at[passed.index(target), phase])
 
     def place(r, target, c):
         f, start, size = cuts[c]
@@ -622,94 +647,82 @@
         block_copy(own, near_y, c, y_dev).start()
         block_copy(own, near_x, c, x_dev).start()
 
-    def supply_inner(f):
-        @pl.when(inner)
-        def _():
-            if f == 0:
-                read_ids()
-
-            def arrived(src, _):
-                row_copy(0, src, f).wait_recv()
-                return 0
-
-            lax.fori_loop(0, groups, arrived, 0)
-            for c in of(f):
-                place(1, deep, c)
-                place(0, own, c)
-                block_copy(deep, own, c, pair_dev).start()
-                share(c)
-            for c in of(f):
-                block_copy(deep, deep_c, c, core_dev).start()
-                block_copy(own, own_c, c, core_dev).start()
+    def arrived(u):
+        f, half_block, size = units[u]
+        landed(got.at[pl.ds(half_block, size), :, lanes[f]], d_recv.at[u])
+
+    def supply_both(f, u):
+        arrived(u)
+        for c in of(f):
+            place(1, deep, c)
+            place(0, own, c)
+            block_copy(deep, own, c, pair_dev).start()
+            share(c)
+            block_copy(deep, deep_c, c, core_dev).start()
+            block_copy(own, own_c, c, core_dev).start()
+
+    def supply_deep(f, u):
+        arrived(u)
+        for c in of(f):
+            place(1, deep, c)
+            block_copy(deep, own, c, pair_dev).start()
+            block_copy(deep, deep_c, c, core_dev).start()
+
+    def supply_own(f, u):
+        arrived(u)
+        for c in of(f):
+            place(0, own, c)
+            share(c)
+            block_copy(own, own_c, c, core_dev).start()
 
     def supply_outer(f):
-        @pl.when(outer)
-        def _():
-            for c in of(f):
-                block_copy(own, own, c, core_dev).wait_recv()
-                share(c)
-                block_copy(own, own_c, c, core_dev).start()
-
-    def supply(f):
-        supply_inner(f)
-        supply_outer(f)
-
-    def forward(f):
+        for c in of(f):
+            block_copy(own, own, c, core_dev).wait_recv()
+            share(c)
+            block_copy(own, own_c, c, core_dev).start()
+
+    def forward(f, within):
         for c in of(f):
             block_copy(own, near_y, c, core_dev).wait_recv()
-
-            @pl.when(jnp.logical_and(inner, right))
-            def _(c=c):
-                block_copy(near_y, skew, c, x_dev).start()
-
-            if f == last:
-                lower(c)
+            if within:
+                if f != 3:
+                    @pl.when(right)
+                    def _(c=c):
+                        block_copy(near_y, skew, c, x_dev).start()
+
+                @pl.when(left)
+                def _(c=c):
+                    block_copy(near_y, deep, c, pair_dev).start()
+
             block_copy(near_y, near_y_c, c, core_dev).start()
             block_copy(own, near_x, c, core_dev).wait_recv()
             block_copy(near_x, near_x_c, c, core_dev).start()
 
-    def lower(*fs):
-        @pl.when(jnp.logical_and(inner, left))
-        def _():
-            for c in fs:
-                block_copy(near_y, deep, c, pair_dev).start()
-
-    def collect_near(f):
-        arrive(own_c, f)
-
-        @pl.when(inner)
-        def _():
-            arrive(deep_c, f)
-
-    def collect_rest(f):
-        arrive(near_x_c, f)
-        arrive(near_y_c, f)
-
-        @pl.when(jnp.logical_and(outer, left))
-        def _():
-            arrive(deep, f)
-
-    inner_jobs = [(own, own_c), (own, deep), (own, deep_c), (own, near_x), (near_x, deep), (near_x, deep_c),
-                  (own, near_y), (near_y, deep), (near_y, deep_c), (near_x, near_y)]
-    outer_jobs = [(own, own_c), (own, near_x), (own, near_y), (near_x, near_y), (deep, near_x), (deep, near_x_c)]
-    inner_early, outer_early = 3, 1
-
-    def shift(a, b):
-        if (a, b) == (own, near_x) or (a, b) == (near_x, near_y):
-            return x
-        return g if (a, b) == (own, near_y) else 0
+    inner_jobs = [(own, own_c), (own, deep), (own, deep_c), (own, near_x + x), (near_x, deep), (near_x, deep_c),
+                  (own, near_y + g), (near_y, deep), (near_y, deep_c), (near_x, near_y + x)]
+    right_jobs = [(own, own_c), (own, near_x + x), (own, near_y + g), (near_x, near_y + x), (near_y_c - x, near_x_c)]
+    left_jobs = right_jobs[:3] + [(deep, near_x), (deep, near_x_c)]
 
     def table(jobs, j):
         a, b = 0, 0
         for n, (p, q) in enumerate(jobs):
             a = a + jnp.where(j == n, p, 0)
-            b = b + jnp.where(j == n, q + shift(p, q), 0)
+            b = b + jnp.where(j == n, q, 0)
         return a, b
 
+    def reduce(scores, a, b, y):
+        xbest[b] = jnp.maximum(xbest[b], jnp.max(scores.reshape(sub // 8, 8, sub), axis=0))
+        if y is None:
+            return
+        side = scores[:, :128]
+        for k in range(1, sub // 128):
+            side = jnp.maximum(side, scores[:, k * 128 : (k + 1) * 128])
+        ybest[y] = jnp.maximum(ybest[y], side)
+
     def tile(a, b, slot, phase, diagonal=False):
-        low, high = phases[phase] if slot is not None else (0, features)
+        low, high = phases[phase]
         scores = dot(raw[a, :, low:high], raw[b, :, low:high], NT)
-        if phase and slot is not None:
+        if phase:
             scores = scores + acc[slot]
         if phase < len(phases) - 1:
             acc[slot] = scores
@@ -720,124 +733,163 @@
                 == lax.broadcasted_iota(jnp.int32, (sub, sub), 1)
             )
             scores = jnp.where(same, -2.0, scores)
-        xbest[b] = jnp.maximum(xbest[b], jnp.max(scores.reshape(sub // 8, 8, sub), axis=0))
-        if diagonal:
-            return
-        side = scores[:, :128]
-        for k in range(1, sub // 128):
-            side = jnp.maximum(side, scores[:, k * 128 : (k + 1) * 128])
-        y = 3 if slot is None else jnp.minimum(a // 2, 2)
-        ybest[y] = jnp.maximum(ybest[y], side)
-
-    def diagonal(phase):
+        reduce(scores, a, b, None if diagonal else jnp.minimum(a // 2, 2))
+
+    def score(phase, within, start, stop):
+        def one(j, _):
+            if within:
+                a, b = table(inner_jobs, j)
+            else:
+                la, lb = table(left_jobs, j)
+                ra, rb = table(right_jobs, j)
+                a, b = jnp.where(left, la, ra), jnp.where(left, lb, rb)
+            tile(a, b, j + 1, phase)
+            return 0
+
+        lax.fori_loop(start, stop, one, 0)
+
+    def score_early(phase, within):
         tile(own, own, 0, phase, True)
-
-    def others(phase, start, stop):
-        def one(j, _):
-            ia, ib = table(inner_jobs, j)
-            oa, ob = table(outer_jobs, j)
-            tile(jnp.where(inner, ia, oa), jnp.where(inner, ib, ob), j + 1, phase)
-            return 0
-
-        lax.fori_loop(start, stop, one, 0)
-
-    skip = jnp.where(inner, core, 1 - core)
-    early = jnp.where(inner, inner_early, outer_early)
-    total = jnp.where(inner, len(inner_jobs), jnp.where(left, len(outer_jobs), len(outer_jobs) - 2))
-
-    def score_early(phase, *fs):
-        for f in fs:
-            collect_near(f)
-        diagonal(phase)
-        others(phase, skip, early)
-
-    def score_late(phase, *fs):
-        for f in fs:
-            collect_rest(f)
-        others(phase, early, total)
-
-    final = len(phases) - 1
-    supply(0)
-    send_y(3)
-    relay(2)
-    send_z(3)
-    supply(1)
-    forward(0)
-    lower(0)
-    send_y(4)
-    relay(3)
-    send_z(4)
+        collect(own_c, phase)
+        if within:
+            collect(deep_c, phase)
+            score(phase, True, core, 3)
+        else:
+            score(phase, False, 1 - core, 1)
+
+    def score_late(phase):
+        collect(near_x_c, phase)
+        collect(near_y_c, phase)
+        score(phase, False, 1, jnp.where(left, 3, 5))
+
+    def score_deep(phase):
+        @pl.when(left)
+        def _():
+            collect(deep, phase)
+            score(phase, False, 3, 5)
+
+    split = phases[0][1]
+
+    def begin_skew():
+        @pl.when(right)
+        def _():
+            collect(skew, 0)
+            acc[1] = dot(raw[skew, :, :split], raw[deep, :, :split], NT)
+
+    def finish_skew():
+        @pl.when(right)
+        def _():
+            for phase in range(1, len(phases)):
+                collect(skew, phase)
+            reduce(dot(raw[skew, :, split:], raw[deep, :, split:], NT) + acc[1], skew, deep, 3)
+            reduce(dot(raw[skew], raw[deep_c], NT), skew, deep_c, 3)
+
+    @pl.when(inner)
+    def _():
+        read_ids()
+        supply_both(0, 0)
+        send_y(4)
+        relay(2)
+        send_z(3)
+        relay(3)
+        send_z(4)
+        supply_both(1, 1)
+        forward(0, True)
+        send_y(5)
+        send_y(6)
+        supply_deep(2, 2)
+        relay(4)
+        send_z(5)
+        forward(1, True)
+        relay(5)
+        send_z(6)
+        supply_own(2, 3)
+        relay(6)
+        send_z(7)
+        send_y(7)
+        send_y(8)
+        send_y(9)
+        score_early(0, True)
+        supply_deep(3, 4)
+        forward(2, True)
+        supply_deep(4, 5)
+        relay(7)
+        send_z(8)
+        relay(8)
+        send_z(9)
+        collect(near_x_c, 0)
+        collect(near_y_c, 0)
+        score(0, True, 3, 10)
+        supply_own(3, 6)
+        relay(9)
+        score_early(1, True)
+        supply_deep(5, 7)
+        begin_skew()
+        supply_own(4, 8)
+        forward(3, True)
+        supply_own(5, 9)
+
+        @pl.when(right)
+        def _():
+            for c in of(3):
+                block_copy(near_x, skew, c, y_dev).start()
+
+        collect(near_x_c, 1)
+        collect(near_y_c, 1)
+        score(1, True, 3, 6)
+        forward(4, True)
+        score(1, True, 6, 10)
+        score_early(2, True)
+        forward(5, True)
+        collect(near_x_c, 2)
+        collect(near_y_c, 2)
+        score(2, True, 3, 10)
+        finish_skew()
 
     @pl.when(outer)
     def _():
+        supply_outer(0)
+        send_y(4)
         send_y(5)
-
-    forward(1)
-    supply(2)
-
-    @pl.when(inner)
-    def _():
-        send_y(5)
-
-    lower(1)
-    score_early(0, 0, 1, 2)
-    relay(4)
-    send_z(5)
-
-    @pl.when(outer)
-    def _():
+        send_y(6)
+        relay(2)
+        send_z(3)
+        relay(3)
+        send_z(4)
+        supply_outer(1)
+        send_y(7)
+        send_y(8)
+        send_y(9)
+        relay(4)
+        send_z(5)
         relay(5)
-
-    forward(2)
-    lower(2)
-
-    @pl.when(inner)
-    def _():
-        relay(5)
-
-    supply(3)
-    supply_outer(4)
-    score_late(0, 0, 1, 2)
-    supply_inner(4)
-    score_early(1, 3)
-    supply_outer(5)
-    forward(3)
-    lower(3)
-    score_late(1, 3)
-    supply_inner(5)
-    forward(4)
-    lower(4)
-    score_early(2, 4, 5)
-    forward(5)
-    score_late(2, 4, 5)
-
-    def score_skew():
-        @pl.when(jnp.logical_and(inner, right))
-        def _():
-            for f in range(last + 1):
-                arrive(skew, f)
-
-            def one(n, _):
-                tile(skew, deep + n, None, final)
-                return 0
-
-            lax.fori_loop(0, 2, one, 0)
-
-    score_skew()
-    tops = []
-    for n in range(4):
-        with_side = jnp.transpose(ybest[n])
-        tops.append(jnp.max(with_side.reshape(16, 8, sub), axis=0))
-    y_of = {own: 0, near_x: 1, skew: 3}
-    for b in range(9):
-        top = tops[3] if b == skew else xbest[b]
-        if b in y_of and b != skew:
-            top = jnp.maximum(top, tops[y_of[b]])
-        if b == near_y:
-            top = jnp.maximum(top, jnp.where(inner, tops[2], -2.0))
-        if b == deep:
-            top = jnp.maximum(top, jnp.where(inner, -2.0, tops[2]))
-        mine[b] = jnp.max(top, axis=0, keepdims=True)
+        send_z(6)
+        relay(6)
+        send_z(7)
+        forward(0, False)
+        forward(1, False)
+        relay(7)
+        send_z(8)
+        relay(8)
+        send_z(9)
+        relay(9)
+        supply_outer(2)
+        score_early(0, False)
+        forward(2, False)
+        supply_outer(3)
+        score_late(0)
+        supply_outer(4)
+        score_early(1, False)
+        forward(3, False)
+        supply_outer(5)
+        score_late(1)
+        score_deep(0)
+        forward(4, False)
+        score_early(2, False)
+        forward(5, False)
+        score_late(2)
+        score_deep(1)
+        score_deep(2)
 
     role = outer.astype(jnp.int32)
 
@@ -871,14 +923,62 @@
             return jnp.logical_or(inner, left)
         return jnp.logical_and(inner, right) if b == skew else True
 
-    for b in range(9):
+    def top_of(n):
+        return jnp.max(jnp.transpose(ybest[n]).reshape(16, 8, sub), axis=0)
+
+    def give(b, top):
+        mine[b] = jnp.max(top, axis=0, keepdims=True)
+
         @pl.when(jnp.logical_and(holds(b), stays(b)))
-        def _(b=b):
+        def _():
             parts[deep if b == skew else b] = mine[b]
 
         @pl.when(jnp.logical_and(holds(b), jnp.logical_not(stays(b))))
-        def _(b=b):
+        def _():
             part_copy(b).start()
+
+    for b in (near_x_c, own_c, deep_c):
+        give(b, xbest[b])
+    give(near_x, jnp.maximum(xbest[near_x], top_of(1)))
+    last_top = top_of(2)
+    crossed = jnp.logical_and(outer, right)
+    for b, mine_too in ((near_y, jnp.logical_or(inner, jnp.logical_and(crossed, x == 1))),
+                        (near_y_c, jnp.logical_and(crossed, x == 0)),
+                        (deep, jnp.logical_and(outer, left))):
+        give(b, jnp.maximum(xbest[b], jnp.where(mine_too, last_top, -2.0)))
+    give(own, jnp.maximum(xbest[own], top_of(0)))
+
+    @pl.when(jnp.logical_and(inner, right))
+    def _():
+        give(skew, top_of(3))
+
+    def drain(o, _):
+        @pl.when(jnp.logical_not(is_me(o)))
+        def _():
+            departed(send_ids.at[pl.ds(o * 2, 2)], i_send.at[o])
+            departed(send.at[o], d_send.at[o])
+        return 0
+
+    lax.fori_loop(0, homes, drain, 0)
+    for half in halves:
+        @pl.when(jnp.logical_not(level(half)))
+        def _(half=half):
+            departed(hop.at[half], h_send.at[half])
+    for target in (near_y, near_x, own_c, near_y_c, near_x_c):
+        departed(raw.at[own], g_send.at[target])
+
+    @pl.when(inner)
+    def _():
+        for target in (own, deep_c):
+            departed(raw.at[own], g_send.at[target])
+
+    @pl.when(jnp.logical_and(inner, left))
+    def _():
+        departed(raw.at[own], g_send.at[deep])
+
+    @pl.when(jnp.logical_and(inner, right))
+    def _():
+        departed(raw.at[own], g_send.at[skew])
 
     half, rr = tj // 2, lax.rem(tj, 2)
 
@@ -919,37 +1019,6 @@
         def _(b=b):
             part_copy(b).wait_send()
 
-    def drain(o, _):
-        @pl.when(jnp.logical_not(is_me(o)))
-        def _():
-            id_copy(o, lin).wait_send()
-            for f in range(last + 1):
-                row_copy(o, lin, f).wait_send()
-        return 0
-
-    lax.fori_loop(0, homes, drain, 0)
-    for half in halves:
-        @pl.when(jnp.logical_not(level(half)))
-        def _(half=half):
-            for f in range(last + 1):
-                relay_copy(half, f).wait_send()
-    for c in range(len(cuts)):
-        for target in (near_y, near_x, own_c, near_y_c, near_x_c):
-            block_copy(own, target, c, core_dev).wait_send()
-
-        @pl.when(inner)
-        def _(c=c):
-            for target in (own, deep_c):
-                block_copy(own, target, c, core_dev).wait_send()
-
-        @pl.when(jnp.logical_and(inner, left))
-        def _(c=c):
-            block_copy(own, deep, c, core_dev).wait_send()
-
-        @pl.when(jnp.logical_and(inner, right))
-        def _(c=c):
-            block_copy(own, skew, c, core_dev).wait_send()
-
 
 def square(corpus, slot_of_row):
     ti_count, tj_count = lax.axis_size("ti"), lax.axis_size("tj")
@@ -963,6 +1032,7 @@
     phases = [(0, 4 * unit), (4 * unit, 6 * unit), (6 * unit, features)]
     n = len(spans)
     cuts = [(f, 0, sub) for f in range(n - 1)] + [(n - 1, 0, sub // 2), (n - 1, sub // 2, sub // 2)]
+    units = [(0, 0, 2), (1, 0, 2), (2, 1, 1), (2, 0, 1), (3, 1, 1), (4, 1, 1), (3, 0, 1), (5, 1, 1), (4, 0, 1), (5, 0, 1)]
     wide_cap = -(-cap // 128) * 128
     jobs = 11
     piece = 256 if count % 256 == 0 else 128
@@ -971,7 +1041,7 @@
     bf16, f32 = jnp.bfloat16, jnp.float32
     return pl.pallas_call(
         functools.partial(
-            square_kernel, (ti_count, tj_count, count, features, sub, cap, spans, cuts, phases)),
+            square_kernel, (ti_count, tj_count, count, features, sub, cap, spans, units, cuts, phases)),
         out_shape=jax.ShapeDtypeStruct((1, sub), f32),
         in_specs=[vmem, pl.BlockSpec(memory_space=pl.ANY)],
         out_specs=vmem,
@@ -992,9 +1062,9 @@
             pltpu.VMEM((4, sub, 128), f32),
             pltpu.VMEM((9, 1, sub), f32),
             pltpu.VMEM((8, 1, sub), f32),
-            dma((count // piece,)),
-            dma((homes, n)), dma((groups, n)), dma((2, n)), dma((2, n)), dma((homes,)), dma((groups,)),
-            dma((9, len(cuts))), dma((9, len(cuts))), dma((9,)), dma((8,)),
+            dma((1,)),
+            dma((homes,)), dma((len(units),)), dma((2,)), dma((2, len(units))), dma((homes,)), dma((1,)),
+            dma((9,)), dma((3, len(cuts))), dma((6, len(phases))), dma((9,)), dma((8,)),
         ],
         compiler_params=pltpu.CompilerParams(
             collective_id=1, has_side_effects=True, vmem_limit_bytes=63 * 1024 * 1024),

time: 104 us -> 102 us (0.981)
    pallas_call x1, Pallas kernels: 102 us -> 101 us  [square(): pl.pallas_call(functools.partial(square_kernel, (ti_count, tj_count, coun...]
where the time goes in v4:
time: 102 us
  Pallas kernels  101 us (99%)
  local copies, waits for them, and re-layouts  1.26 us (1%)
    pallas_call x1, Pallas kernels, square(): pl.pallas_call(functools.partial(square_kernel, (ti_count, tj_count, coun...  101 us

profile of v4, /device:TPU:0, one launch (start us, length us, event | category | flops | bytes accessed | tf_op | source)
XLA Modules:
  0.0 101.9 jit_solution(13106818795290275149)
XLA Ops:
  0.0 100.6 %shard_map.28 = f32[1,768]{1,0:T(1,128)} custom-call(s32[1,1536]{1,0:T(1,128)} %slots_ref.1, bf16[1,1536,1024]{2,1,0:T(8,128)(2,1)} %corpus_ref.1), custom_call_target="tpu_custom_call" | custom-call | tf_op jit(solution)/shard_map/pallas_call | solution.py:1042
  100.6 1.3 %copy.4 = f32[1,768]{1,0:T(1,128)} copy(f32[1,768]{1,0:T(1,128)} %shard_map.28) | data formatting | bytes 6144

commit v5 on v4

--- a/solution.py
+++ b/solution.py
@@ -690,16 +690,17 @@
                     def _(c=c):
                         block_copy(near_y, skew, c, x_dev).start()
 
-                @pl.when(left)
-                def _(c=c):
-                    block_copy(near_y, deep, c, pair_dev).start()
+                if f != last:
+                    @pl.when(left)
+                    def _(c=c):
+                        block_copy(near_y, deep, c, pair_dev).start()
 
             block_copy(near_y, near_y_c, c, core_dev).start()
             block_copy(own, near_x, c, core_dev).wait_recv()
             block_copy(near_x, near_x_c, c, core_dev).start()
 
-    inner_jobs = [(own, own_c), (own, deep), (own, deep_c), (own, near_x + x), (near_x, deep), (near_x, deep_c),
-                  (own, near_y + g), (near_y, deep), (near_y, deep_c), (near_x, near_y + x)]
+    inner_jobs = [(own, own_c), (own, deep), (own, deep_c), (near_x, deep), (near_x, deep_c), (near_y, deep), (near_y, deep_c),
+                  (own, near_x + x), (own, near_y + g), (near_x, near_y + x)]
     right_jobs = [(own, own_c), (own, near_x + x), (own, near_y + g), (near_x, near_y + x), (near_y_c - x, near_x_c)]
     left_jobs = right_jobs[:3] + [(deep, near_x), (deep, near_x_c)]
 
@@ -826,24 +827,39 @@
         supply_deep(5, 7)
         begin_skew()
         supply_own(4, 8)
-        forward(3, True)
+
+        @pl.when(right)
+        def _():
+            forward(3, True)
+
         supply_own(5, 9)
+
+        @pl.when(left)
+        def _():
+            forward(3, True)
+
+        score(1, True, 3, 7)
 
         @pl.when(right)
         def _():
             for c in of(3):
                 block_copy(near_x, skew, c, y_dev).start()
 
+        @pl.when(left)
+        def _():
+            for c in of(last):
+                block_copy(own, deep, c, dev(1 - g, ti, zh * 2 + 1 - zl)).start()
+
+        forward(4, True)
         collect(near_x_c, 1)
         collect(near_y_c, 1)
-        score(1, True, 3, 6)
-        forward(4, True)
-        score(1, True, 6, 10)
+        score(1, True, 7, 10)
         score_early(2, True)
         forward(5, True)
+        score(2, True, 3, 7)
         collect(near_x_c, 2)
         collect(near_y_c, 2)
-        score(2, True, 3, 10)
+        score(2, True, 7, 10)
         finish_skew()
 
     @pl.when(outer)

time: 102 us -> 99.6 us (0.976)
  Pallas kernels: 101 us -> 97.8 us
    pallas_call x1, Pallas kernels: 101 us -> 97.8 us  [square(): pl.pallas_call(functools.partial(square_kernel, (ti_count, tj_count, coun...]
where the time goes in v5:
time: 99.6 us; the launch traced here: 99.1 us
  Pallas kernels  97.8 us (98%)
  local copies, waits for them, and re-layouts  1.26 us (1%)
    pallas_call x1, Pallas kernels, square(): pl.pallas_call(functools.partial(square_kernel, (ti_count, tj_count, coun...  97.8 us

profile of v5, /device:TPU:0, one launch (start us, length us, event | category | flops | bytes accessed | tf_op | source)
XLA Modules:
  0.0 99.1 jit_solution(823424111147640524)
XLA Ops:
  0.0 97.8 %shard_map.28 = f32[1,768]{1,0:T(1,128)} custom-call(s32[1,1536]{1,0:T(1,128)} %slots_ref.1, bf16[1,1536,1024]{2,1,0:T(8,128)(2,1)} %corpus_ref.1), custom_call_target="tpu_custom_call" | custom-call | tf_op jit(solution)/shard_map/pallas_call | solution.py:1058
  97.8 1.3 %copy.4 = f32[1,768]{1,0:T(1,128)} copy(f32[1,768]{1,0:T(1,128)} %shard_map.28) | data formatting | bytes 6144

commit v6 on v5

--- a/solution.py
+++ b/solution.py
@@ -784,6 +784,52 @@
                 collect(skew, phase)
             reduce(dot(raw[skew, :, split:], raw[deep, :, split:], NT) + acc[1], skew, deep, 3)
             reduce(dot(raw[skew], raw[deep_c], NT), skew, deep_c, 3)
+
+    role = outer.astype(jnp.int32)
+
+    def final_dev(b):
+        dx, dc, dg = b in (near_x, near_x_c, skew), b in (own_c, near_x_c, near_y_c, deep_c), b in (near_y, near_y_c, skew)
+        gg = 1 - g if dg else g
+        rr = role
+        if b == deep:
+            gg = jnp.where(inner, g, 1 - g)
+        if b in (deep, deep_c):
+            rr = 1 - role
+        xx = 1 - x if dx else x
+        cc = 1 - core if dc else core
+        return zh, xx * CORES + cc, gg * 2 + rr
+
+    def part_copy(b):
+        gg, tt, jj = final_dev(b)
+        return pltpu.make_async_remote_copy(
+            mine.at[b], parts.at[deep if b == skew else b], p_send.at[b],
+            p_recv.at[deep if b == skew else b],
+            device_id=dev(gg, tt, jj), device_id_type=MESH)
+
+    def stays(b):
+        gg, tt, jj = final_dev(b)
+        return jnp.logical_and(gg == g, jnp.logical_and(tt == ti, jj == tj))
+
+    def holds(b):
+        if b == deep_c:
+            return inner
+        if b == deep:
+            return jnp.logical_or(inner, left)
+        return jnp.logical_and(inner, right) if b == skew else True
+
+    def top_of(n):
+        return jnp.max(jnp.transpose(ybest[n]).reshape(16, 8, sub), axis=0)
+
+    def give(b, top):
+        mine[b] = jnp.max(top, axis=0, keepdims=True)
+
+        @pl.when(jnp.logical_and(holds(b), stays(b)))
+        def _():
+            parts[deep if b == skew else b] = mine[b]
+
+        @pl.when(jnp.logical_and(holds(b), jnp.logical_not(stays(b))))
+        def _():
+            part_copy(b).start()
 
     @pl.when(inner)
     def _():
@@ -860,7 +906,17 @@
         collect(near_x_c, 2)
         collect(near_y_c, 2)
         score(2, True, 7, 10)
+        for b in (own_c, near_x_c, near_y_c):
+            give(b, xbest[b])
+        for b in (own, near_x, near_y):
+            give(b, jnp.maximum(xbest[b], top_of(b // 2)))
         finish_skew()
+        for b in (deep, deep_c):
+            give(b, xbest[b])
+
+        @pl.when(right)
+        def _():
+            give(skew, top_of(3))
 
     @pl.when(outer)
     def _():
@@ -904,69 +960,19 @@
         score_early(2, False)
         forward(5, False)
         score_late(2)
+        give(own_c, xbest[own_c])
+        give(own, jnp.maximum(xbest[own], top_of(0)))
+        crossed = top_of(2)
+        for b, mine_too in ((near_y, jnp.logical_and(right, x == 1)), (near_y_c, jnp.logical_and(right, x == 0))):
+            give(b, jnp.maximum(xbest[b], jnp.where(mine_too, crossed, -2.0)))
         score_deep(1)
         score_deep(2)
-
-    role = outer.astype(jnp.int32)
-
-    def final_dev(b):
-        dx, dc, dg = b in (near_x, near_x_c, skew), b in (own_c, near_x_c, near_y_c, deep_c), b in (near_y, near_y_c, skew)
-        gg = 1 - g if dg else g
-        rr = role
-        if b == deep:
-            gg = jnp.where(inner, g, 1 - g)
-        if b in (deep, deep_c):
-            rr = 1 - role
-        xx = 1 - x if dx else x
-        cc = 1 - core if dc else core
-        return zh, xx * CORES + cc, gg * 2 + rr
-
-    def part_copy(b):
-        gg, tt, jj = final_dev(b)
-        return pltpu.make_async_remote_copy(
-            mine.at[b], parts.at[deep if b == skew else b], p_send.at[b],
-            p_recv.at[deep if b == skew else b],
-            device_id=dev(gg, tt, jj), device_id_type=MESH)
-
-    def stays(b):
-        gg, tt, jj = final_dev(b)
-        return jnp.logical_and(gg == g, jnp.logical_and(tt == ti, jj == tj))
-
-    def holds(b):
-        if b == deep_c:
-            return inner
-        if b == deep:
-            return jnp.logical_or(inner, left)
-        return jnp.logical_and(inner, right) if b == skew else True
-
-    def top_of(n):
-        return jnp.max(jnp.transpose(ybest[n]).reshape(16, 8, sub), axis=0)
-
-    def give(b, top):
-        mine[b] = jnp.max(top, axis=0, keepdims=True)
-
-        @pl.when(jnp.logical_and(holds(b), stays(b)))
+        give(near_x_c, xbest[near_x_c])
+        give(near_x, jnp.maximum(xbest[near_x], top_of(1)))
+
+        @pl.when(left)
         def _():
-            parts[deep if b == skew else b] = mine[b]
-
-        @pl.when(jnp.logical_and(holds(b), jnp.logical_not(stays(b))))
-        def _():
-            part_copy(b).start()
-
-    for b in (near_x_c, own_c, deep_c):
-        give(b, xbest[b])
-    give(near_x, jnp.maximum(xbest[near_x], top_of(1)))
-    last_top = top_of(2)
-    crossed = jnp.logical_and(outer, right)
-    for b, mine_too in ((near_y, jnp.logical_or(inner, jnp.logical_and(crossed, x == 1))),
-                        (near_y_c, jnp.logical_and(crossed, x == 0)),
-                        (deep, jnp.logical_and(outer, left))):
-        give(b, jnp.maximum(xbest[b], jnp.where(mine_too, last_top, -2.0)))
-    give(own, jnp.maximum(xbest[own], top_of(0)))
-
-    @pl.when(jnp.logical_and(inner, right))
-    def _():
-        give(skew, top_of(3))
+            give(deep, jnp.maximum(xbest[deep], top_of(2)))
 
     def drain(o, _):
         @pl.when(jnp.logical_not(is_me(o)))

time: 99.6 us -> 99.5 us (level)
  no operation moved by 1% of the time
where the time goes in v6:
time: 99.5 us; the launch traced here: 98.7 us
  Pallas kernels  97.4 us (98%)
  local copies, waits for them, and re-layouts  1.26 us (1%)
    pallas_call x1, Pallas kernels, square(): pl.pallas_call(functools.partial(square_kernel, (ti_count, tj_count, coun...  97.4 us

profile of v6, /device:TPU:0, one launch (start us, length us, event | category | flops | bytes accessed | tf_op | source)
XLA Modules:
  0.0 98.7 jit_solution(11864604497829951262)
XLA Ops:
  0.0 97.4 %shard_map.28 = f32[1,768]{1,0:T(1,128)} custom-call(s32[1,1536]{1,0:T(1,128)} %slots_ref.1, bf16[1,1536,1024]{2,1,0:T(8,128)(2,1)} %corpus_ref.1), custom_call_target="tpu_custom_call" | custom-call | tf_op jit(solution)/shard_map/pallas_call | solution.py:1064
  97.4 1.3 %copy.4 = f32[1,768]{1,0:T(1,128)} copy(f32[1,768]{1,0:T(1,128)} %shard_map.28) | data formatting | bytes 6144

commit v7 on v6

--- a/solution.py
+++ b/solution.py
@@ -878,11 +878,20 @@
         def _():
             forward(3, True)
 
+        @pl.when(left)
+        def _():
+            for c in of(3):
+                block_copy(own, near_y, c, core_dev).wait_recv()
+                block_copy(near_y, deep, c, pair_dev).start()
+                block_copy(near_y, near_y_c, c, core_dev).start()
+
         supply_own(5, 9)
 
         @pl.when(left)
         def _():
-            forward(3, True)
+            for c in of(3):
+                block_copy(own, near_x, c, core_dev).wait_recv()
+                block_copy(near_x, near_x_c, c, core_dev).start()
 
         score(1, True, 3, 7)
 

time: 99.5 us -> 99.5 us (level)
  no operation moved by 1% of the time
where the time goes in v7:
time: 99.5 us; the launch traced here: 98.6 us
  Pallas kernels  97.4 us (98%)
  local copies, waits for them, and re-layouts  1.26 us (1%)
    pallas_call x1, Pallas kernels, square(): pl.pallas_call(functools.partial(square_kernel, (ti_count, tj_count, coun...  97.4 us

profile of v7, /device:TPU:0, one launch (start us, length us, event | category | flops | bytes accessed | tf_op | source)
XLA Modules:
  0.0 98.6 jit_solution(9091920314359915583)
XLA Ops:
  0.0 97.4 %shard_map.28 = f32[1,768]{1,0:T(1,128)} custom-call(s32[1,1536]{1,0:T(1,128)} %slots_ref.1, bf16[1,1536,1024]{2,1,0:T(8,128)(2,1)} %corpus_ref.1), custom_call_target="tpu_custom_call" | custom-call | tf_op jit(solution)/shard_map/pallas_call | solution.py:1073
  97.4 1.3 %copy.4 = f32[1,768]{1,0:T(1,128)} copy(f32[1,768]{1,0:T(1,128)} %shard_map.28) | data formatting | bytes 6144
